TPU v7x, 256 devices: a whole 4x4x8 slice. The times are simulated.
256 devices in a mesh: env: 4 (over x_lo, core), tm: 64 (over x_hi, z, y).
Axes of the slice: x: 4 (x_hi: 2, x_lo: 2; x = x_hi * 2 + x_lo), y: 4, z: 8, core: 2. Of those that a mesh axis runs over, the one named last changes fastest.
Arguments:
- hidden: bfloat16 [4, 64, 256, 1024], P('env', 'tm'), may hold values from -6 to 6
- done_step: int32 [4, 64], P('env', 'tm'), may hold values from 0 to 255
- alive: int32 [4, 64, 256], P('env', None, 'tm'), may hold values 0 or 1
- targets: float32 [4, 64, 256], P('env', None, 'tm'), may hold values from -6 to 6
- gain_t: float32 [1024], replicated, may hold values from 0.25 to 1.75
- w_qkv_t: bfloat16 [1024, 3072], replicated, may hold values from -5 to 5
- w_out_t: bfloat16 [1024, 1024], replicated, may hold values from -0.1875 to 0.1875
- gain_a: float32 [1024], replicated, may hold values from 0.25 to 1.75
- w_qkv_a: bfloat16 [1024, 3072], P('tm'), may hold values from -5 to 5
- w_out_a: bfloat16 [1024, 1024], P('tm'), may hold values from -0.1875 to 0.1875
- w_value: float32 [1024], replicated, may hold values from -0.1875 to 0.1875
Outputs:
- values: float32 [4, 64, 256], P('env', None, 'tm')
- input_grad: bfloat16 [4, 64, 256, 1024], P('env', 'tm')
- qkv_grad: float32 [1024, 3072], P('tm')
- out_grad: float32 [1024, 1024], P('tm')
Inputs may be any that keep to these rules, and one draw needn't show every extreme that they name: `done_step`: the last step of an agent's first episode in the window; later steps form a new episode.
All inputs are finite; a program needn't handle non-finite values. No bound on the sum of `alive` on one device may be relied on, other than what follows from the above.
Results may differ from a plain program's by a relative error of at most 0.02.
Values may be sent and summed in bfloat16 or wider, within the bound.
A program may use at most 128 MiB of HBM per device.

v0:
```python
import math

import jax
import jax.numpy as jnp
from jax import lax
from jax.sharding import PartitionSpec as P

HEADS = 8


def norm_scale(rows, gain):
    return rows * lax.rsqrt(jnp.mean(rows * rows, axis=-1, keepdims=True) + 1e-06) * gain


def attend(qkv, allowed, head_count, layout):
    width = qkv.shape[-1] // 3
    size = width // head_count
    shape = qkv.shape[:-1] + (head_count, size)
    queries = qkv[..., :width].reshape(shape).astype(jnp.float32)
    key_rows = qkv[..., width : 2 * width].reshape(shape).astype(jnp.float32)
    value_rows = qkv[..., 2 * width :].reshape(shape).astype(jnp.float32)
    if layout == "temporal":
        score_form = "bqhe,bkhe->bhqk"
        mix_form = "bhqk,bkhe->bqhe"
    else:
        score_form = "qbhe,kbhe->bhqk"
        mix_form = "bhqk,kbhe->qbhe"
    scores = jnp.einsum(score_form, queries, key_rows) / math.sqrt(size)
    scores = jnp.where(allowed[:, None], scores, -1e30)
    row_max = jnp.max(scores, axis=-1, keepdims=True)
    weights = jnp.exp(scores - row_max)
    probs = (weights / jnp.sum(weights, axis=-1, keepdims=True)).astype(jnp.bfloat16)
    mixed = jnp.einsum(mix_form, probs.astype(jnp.float32), value_rows)
    return mixed.reshape(qkv.shape[:-1] + (width,))


def temporal_block(rows, done, gain, w_qkv, w_out, head_count):
    batch, length, width = rows.shape
    rows_f = rows.astype(jnp.float32)
    normed = norm_scale(rows_f, gain).astype(jnp.bfloat16)
    qkv = jnp.dot(normed.reshape(-1, width), w_qkv, preferred_element_type=jnp.float32)
    qkv = qkv.astype(jnp.bfloat16).reshape(batch, length, 3 * width)
    positions = jnp.arange(length, dtype=jnp.int32)
    later = positions[None, :] > done[:, None]
    causal = positions[:, None] >= positions[None, :]
    allowed = causal[None] & (later[:, :, None] == later[:, None, :])
    mixed = attend(qkv, allowed, head_count, "temporal").astype(jnp.bfloat16)
    added = jnp.dot(mixed.reshape(-1, width), w_out, preferred_element_type=jnp.float32)
    return (rows_f + added.reshape(batch, length, width)).astype(jnp.bfloat16)


def left_product(left, right):
    return lax.dot_general(
        left, right, (((0,), (0,)), ((), ())), preferred_element_type=jnp.float32
    )


def agent_step(lifted, alive_rows, target_rows, gain, w_qkv, w_out, w_value, head_count):
    agent_count, step_count, width = lifted.shape
    lifted_f = lifted.astype(jnp.float32)
    normed_f, norm_pull = jax.vjp(lambda rows: norm_scale(rows, gain), lifted_f)
    normed = normed_f.astype(jnp.bfloat16).reshape(-1, width)
    qkv = jnp.dot(normed, w_qkv, preferred_element_type=jnp.float32)
    qkv = qkv.astype(jnp.bfloat16).reshape(agent_count, step_count, 3 * width)
    living = alive_rows.T == 1
    allowed = living[:, None, :] | jnp.eye(agent_count, dtype=bool)[None]
    mixed_f, attend_pull = jax.vjp(lambda block: attend(block, allowed, head_count, "agents"), qkv)
    mixed = mixed_f.astype(jnp.bfloat16).reshape(-1, width)
    added = jnp.dot(mixed, w_out, preferred_element_type=jnp.float32)
    top_rows = lifted_f + added.reshape(agent_count, step_count, width)
    predicted = jnp.sum(top_rows * w_value, axis=-1)
    residual_err = 32.0 * alive_rows.astype(jnp.float32) * (predicted - target_rows)
    grad_top = residual_err[..., None] * w_value
    grad_rows = grad_top.astype(jnp.bfloat16).reshape(-1, width)
    grad_mixed = jnp.dot(grad_rows, w_out.T, preferred_element_type=jnp.float32)
    grad_qkv = attend_pull(grad_mixed.reshape(agent_count, step_count, width))[0]
    grad_qkv = grad_qkv.reshape(-1, 3 * width)
    grad_normed = jnp.dot(grad_qkv, w_qkv.T, preferred_element_type=jnp.float32)
    grad_lifted = grad_top + norm_pull(grad_normed.reshape(agent_count, step_count, width))[0]
    return (predicted, grad_lifted.astype(jnp.bfloat16), normed, grad_qkv, mixed, grad_rows)


def per_device(
    hidden, done_step, alive, targets, gain_t, w_qkv_t, w_out_t, gain_a, w_qkv_a, w_out_a, w_value
):
    width = hidden.shape[-1]
    local_rows = hidden[0]
    done_rows = done_step[0]
    first, pull = jax.vjp(
        lambda rows: temporal_block(rows, done_rows, gain_t, w_qkv_t, w_out_t, HEADS), local_rows
    )
    lifted = lax.all_to_all(first, "tm", split_axis=1, concat_axis=0, tiled=True)
    qkv_full, out_full = (
        lax.all_gather(w_qkv_a, "tm", axis=0, tiled=True),
        lax.all_gather(w_out_a, "tm", axis=0, tiled=True),
    )
    predicted, grad_lifted, normed, grad_qkv, mixed, grad_rows = agent_step(
        lifted, alive[0], targets[0], gain_a, qkv_full, out_full, w_value, HEADS
    )
    terms = jnp.concatenate(
        [left_product(normed, grad_qkv), left_product(mixed, grad_rows)], axis=1
    )
    summed = lax.psum_scatter(terms, "tm", scatter_dimension=0, tiled=True)
    totals = lax.psum(summed.astype(jnp.bfloat16), "env").astype(jnp.float32)
    qkv_grad = totals[:, : 3 * width]
    out_grad = totals[:, 3 * width :]
    returned = lax.all_to_all(grad_lifted, "tm", split_axis=0, concat_axis=1, tiled=True)
    input_grad = pull(returned)[0]
    return (predicted[None], input_grad[None], qkv_grad, out_grad)


def solution(mesh):
    in_specs = (
        P("env", "tm", None, None),
        P("env", "tm"),
        P("env", None, "tm"),
        P("env", None, "tm"),
        P(),
        P(),
        P(),
        P(),
        P("tm", None),
        P("tm", None),
        P(),
    )
    out_specs = (P("env", None, "tm"), P("env", "tm", None, None), P("tm", None), P("tm", None))
    return jax.shard_map(
        per_device, mesh=mesh, in_specs=in_specs, out_specs=out_specs, check_vma=False
    )
```

profile of v0, /device:TPU:1, one launch (start us, length us, event | category | flops | bytes accessed | tf_op | source)
XLA Modules:
  0.0 746.1 jit_solution(15809563214694229206)
XLA Ops:
  9.3 1.2 fusion.59
  10.7 4.9 fusion.2
  15.5 0.9 slice_bitcast_fusion
  16.5 0.9 copy.161
  17.6 1.4 copy.155
  22.5 1.9 copy.206
  24.9 5.6 reduce.17
  30.4 2.2 reshape.471
  32.6 15.4 %all-to-all-start = ((bf16[64,2,2048]{2,1,0:T(2,128)(2,1)}), bf16[64,2,2048]{2,1,0:T(2,128)(2,1)}, u32[]{:S(2)}, u32[]{:S(2)}) async-start(bf16[64,2,2048]{2,1,0:T(2,128)(2,1)} %reshape.471), calls=%async_computation | async-start | bytes 1048576 | tf_op jit(solution)/shard_map/all_to_all | solution.py:92
  48.7 16.4 %all-to-all-done = bf16[64,2,2048]{2,1,0:T(2,128)(2,1)} async-done(((bf16[64,2,2048]{2,1,0:T(2,128)(2,1)}), bf16[64,2,2048]{2,1,0:T(2,128)(2,1)}, u32[]{:S(2)}, u32[]{:S(2)}) %all-to-all-start) | async-done | bytes 524320 | tf_op jit(solution)/shard_map/all_to_all | solution.py:92
  65.0 4.5 reshape.472
  69.5 6.9 multiply_reduce_fusion.1
  76.6 2.6 reshape.459
  79.1 3.3 bitcast_convert_fusion
  82.4 69.5 %all-gather.3.cloned.1.call-done = bf16[1024,3072]{1,0:T(8,128)(2,1)} async-done(((bf16[16,3072]{1,0:T(8,128)(2,1)}), bf16[1024,3072]{1,0:T(8,128)(2,1)}) %all-gather.3.cloned.1.call-update) | async-done | bytes 6291472 | tf_op jit(solution)/shard_map/all_gather | solution.py:94
  151.9 6.2 convolution_convert_fusion
  158.1 4.0 reshape.445
  162.1 2.9 fusion.129
  164.9 2.0 reshape.469
  167.0 2.0 reshape.468
  169.0 2.0 reshape.470
  171.0 1.9 fusion.132
  173.2 0.8 copy-done.3
  174.0 1.3 fusion.50
  175.2 95.3 %all-gather.5.cloned.1.call-done = bf16[1024,1024]{1,0:T(8,128)(2,1)} async-done(((bf16[16,1024]{1,0:T(8,128)(2,1)}), bf16[1024,1024]{1,0:T(8,128)(2,1)}) %all-gather.5.cloned.1.call-update) | async-done | bytes 2097168 | tf_op jit(solution)/shard_map/all_gather | solution.py:95
  270.5 3.3 fusion.44
  280.9 0.9 slice-done.3
  282.0 3.5 multiply_reduce_fusion
  285.5 2.5 convolution_bitcast_fusion
  288.0 6.0 pad_maximum_fusion
  294.1 2.2 fusion.60
  296.3 1.2 copy.124
  297.5 7.9 %all-to-all-start.1 = ((bf16[64,4,1024]{2,1,0:T(4,128)(2,1)}), bf16[64,4,1024]{2,1,0:T(4,128)(2,1)}, u32[]{:S(2)}, u32[]{:S(2)}) async-start(bf16[64,4,1024]{2,1,0:T(4,128)(2,1)} %copy.124), calls=%async_computation.1 | async-start | bytes 1048576 | tf_op jit(solution)/shard_map/all_to_all | solution.py:107
  305.5 19.2 %all-to-all-done.1 = bf16[64,4,1024]{2,1,0:T(4,128)(2,1)} async-done(((bf16[64,4,1024]{2,1,0:T(4,128)(2,1)}), bf16[64,4,1024]{2,1,0:T(4,128)(2,1)}, u32[]{:S(2)}, u32[]{:S(2)}) %all-to-all-start.1) | async-done | bytes 524320 | tf_op jit(solution)/shard_map/all_to_all | solution.py:107
  324.8 2.0 all_to_all.8
  326.7 2.6 convolution_convert_fusion.5
  329.3 2.1 copy.142
  331.4 2.7 fusion.6
  334.1 1.0 convert_reduce_fusion
  335.6 1.2 fusion.33
  336.9 1.2 fusion.32
  339.1 2.9 fusion.58
  341.9 309.4 %reduce-scatter.2.cloned.1.call-done = f32[16,4096]{1,0:T(8,128)} async-done(((f32[1024,4096]{1,0:T(8,128)}), f32[16,4096]{1,0:T(8,128)}) %reduce-scatter.2.cloned.1.call-update) | async-done | bytes 262160 | tf_op jit(solution)/shard_map/reduce_scatter | solution.py:103
  651.4 1.6 convert_element_type.264
  653.0 2.3 fusion.76
  655.4 81.0 %all-reduce.8.cloned.1.call-done = bf16[16,4096]{1,0:T(8,128)(2,1)} async-done(((bf16[16,4096]{1,0:T(8,128)(2,1)}), bf16[16,4096]{1,0:T(8,128)(2,1)}) %all-reduce.8.cloned.1.call-update) | async-done | bytes 131088 | tf_op jit(solution)/shard_map/psum | solution.py:104
  736.4 1.4 slice.39
  737.8 1.6 slice.38
  (106 shorter events, 15.4 us)
Async XLA Ops:
  7.2 14.6 %copy-start = (bf16[1024,1024]{1,0:T(8,128)(2,1)S(1)}, bf16[1024,1024]{1,0:T(8,128)(2,1)}, u32[]{:S(2)}) copy-start(bf16[1024,1024]{1,0:T(8,128)(2,1)} %param.17) | copy-start | bytes 6291460
  7.2 144.7 %all-gather.3.cloned.1.call-start = ((), (), s32[]{:S(2)}) async-start(), calls=%async_computation.3 | async-start | bytes 6389760 | tf_op jit(solution)/shard_map/all_gather | solution.py:94
  7.9 262.6 %all-gather.5.cloned.1.call-start = ((), (), s32[]{:S(2)}) async-start(), calls=%async_computation.4 | async-start | bytes 2129920 | tf_op jit(solution)/shard_map/all_gather | solution.py:95
  17.6 2.0 copy-start.10
  19.0 0.8 copy-start.12
  19.6 1.3 copy-start.1
  20.1 1.2 copy-start.7
  20.1 1.6 copy-start.5
  24.3 24.2 %copy-start.19 = (s32[1,64,4]{1,2,0:T(4,128)S(1)}, s32[1,64,4]{1,2,0:T(4,128)}, u32[]{:S(2)}) copy-start(s32[1,64,4]{1,2,0:T(4,128)} %param.13) | copy-start | bytes 3076
  32.6 32.4 %all-to-all-start = ((bf16[64,2,2048]{2,1,0:T(2,128)(2,1)}), bf16[64,2,2048]{2,1,0:T(2,128)(2,1)}, u32[]{:S(2)}, u32[]{:S(2)}) async-start(bf16[64,2,2048]{2,1,0:T(2,128)(2,1)} %reshape.471), calls=%async_computation | async-start | bytes 1048576 | tf_op jit(solution)/shard_map/all_to_all | solution.py:92
  48.0 603.4 %reduce-scatter.2.cloned.1.call-start = ((), (), s32[]{:S(2)}) async-start(), calls=%async_computation.5 | async-start | bytes 17039360 | tf_op jit(solution)/shard_map/reduce_scatter | solution.py:103
  76.6 75.3 %copy-start.24 = (f32[1024]{0:T(1024)S(1)}, f32[1024]{0:T(1024)}, u32[]{:S(2)}) copy-start(f32[1024]{0:T(1024)} %param.18) | copy-start | bytes 12292
  171.0 2.9 copy-start.15
  172.9 1.1 copy-start.3
  174.0 96.6 %copy-start.20 = (f32[1024]{0:T(1024)S(1)}, f32[1024]{0:T(1024)}, u32[]{:S(2)}) copy-start(f32[1024]{0:T(1024)} %param.21) | copy-start | bytes 12292
  175.2 98.6 %copy-start.21 = (f32[1,64,4]{1,2,0:T(4,128)S(1)}, f32[1,64,4]{1,2,0:T(4,128)}, u32[]{:S(2)}) copy-start(f32[1,64,4]{1,2,0:T(4,128)} %param.14) | copy-start | bytes 3076
  270.5 3.4 copy-start.23
  273.9 1.6 copy-start.22
  273.9 1.2 copy-start.4
  275.1 1.0 copy-start.16
  276.2 1.4 copy-start.18
  277.5 1.0 copy-start.17
  278.6 1.0 copy-start.26
  278.6 2.4 slice-start.2
  279.6 2.2 slice-start.3
  280.4 1.6 copy-start.9
  297.5 27.2 %all-to-all-start.1 = ((bf16[64,4,1024]{2,1,0:T(4,128)(2,1)}), bf16[64,4,1024]{2,1,0:T(4,128)(2,1)}, u32[]{:S(2)}, u32[]{:S(2)}) async-start(bf16[64,4,1024]{2,1,0:T(4,128)(2,1)} %copy.124), calls=%async_computation.1 | async-start | bytes 1048576 | tf_op jit(solution)/shard_map/all_to_all | solution.py:107
  305.4 430.9 %all-reduce.8.cloned.1.call-start = ((), (), s32[]{:S(2)}) async-start(), calls=%async_computation.6 | async-start | bytes 262144 | tf_op jit(solution)/shard_map/psum | solution.py:104
  331.4 2.7 copy-start.2
  334.1 1.0 copy-start.8
  334.1 1.5 copy-start.11
  335.6 1.2 copy-start.13
  335.6 2.4 slice-start
  336.9 1.5 copy-start.6
  336.9 2.2 slice-start.1
  336.9 2.2 copy-start.25
  339.1 313.9 %copy-start.14 = (bf16[256,1024]{1,0:T(8,128)(2,1)S(1)}, bf16[256,1024]{1,0:T(8,128)(2,1)}, u32[]{:S(2)}) copy-start(bf16[256,1024]{1,0:T(8,128)(2,1)} %all_to_all.8) | copy-start | bytes 1572868
Sparse Core Ops, SparseCore 0:
  11.7 140.1 all-gather.2
  155.5 114.9 all-gather.4
  294.2 357.0 reduce-scatter.1
  654.4 81.9 all-reduce.7
where the time goes:
time: 755 us; the launch traced here: 746 us
  waiting for transfers between devices  592 us (78%)
  local copies, waits for them, and re-layouts  42.7 us (6%)
  matrix products  40 us (5%)
  other arithmetic  32.1 us (4%)
  starting transfers between devices  23.9 us (3%)
  between operations  15.2 us (2%)
    reduce_scatter x1, waiting for transfers between devices, per_device(): summed = lax.psum_scatter(terms, 'tm', scatter_dimension=0, tiled=True)  309 us
    all_gather x1, waiting for transfers between devices, per_device(): lax.all_gather(w_out_a, 'tm', axis=0, tiled=True)  95.3 us
    psum x1, waiting for transfers between devices, per_device(): totals = lax.psum(summed.astype(jnp.bfloat16), 'env').astype(jnp.float32)  81 us
    all_gather x1, waiting for transfers between devices, per_device(): lax.all_gather(w_qkv_a, 'tm', axis=0, tiled=True)  69.5 us
    all_to_all x1, waiting for transfers between devices, per_device(): lax.all_to_all(grad_lifted, 'tm', split_axis=0, concat_axis=1, tiled=True)  19.2 us
    all_to_all x1, waiting for transfers between devices, per_device(): lax.all_to_all(first, 'tm', split_axis=1, concat_axis=0, tiled=True)  16.4 us
    all_to_all x1, starting transfers between devices, per_device(): lax.all_to_all(first, 'tm', split_axis=1, concat_axis=0, tiled=True)  15.4 us
  transfers between devices with their start and end apart: 6, of which 6 were waited for; matrix products, arithmetic and copies ran while one was open for 11% of the time, Pallas kernels for 0%

commit v1 on v0

v1 whole, which is shorter than its diff:
```python
import math

import jax
import jax.numpy as jnp
from jax import lax
from jax.sharding import PartitionSpec as P

HEADS = 8
HI = lax.Precision.HIGHEST


def norm_scale(rows, gain):
    return rows * lax.rsqrt(jnp.mean(rows * rows, axis=-1, keepdims=True) + 1e-06) * gain


def attend(qkv, allowed, head_count):
    width = qkv.shape[-1] // 3
    size = width // head_count
    shape = qkv.shape[:-1] + (head_count, size)
    queries = qkv[..., :width].reshape(shape)
    key_rows = qkv[..., width : 2 * width].reshape(shape)
    value_rows = qkv[..., 2 * width :].reshape(shape)
    scores = jnp.einsum("qhe,khe->hqk", queries, key_rows, preferred_element_type=jnp.float32)
    scores = jnp.where(allowed[None], scores / math.sqrt(size), -1e30)
    row_max = jnp.max(scores, axis=-1, keepdims=True)
    weights = jnp.exp(scores - row_max)
    probs = (weights / jnp.sum(weights, axis=-1, keepdims=True)).astype(jnp.bfloat16)
    mixed = jnp.einsum("hqk,khe->qhe", probs, value_rows, preferred_element_type=jnp.float32)
    return mixed.reshape(qkv.shape[:-1] + (width,))


def temporal_block(rows, done, gain, w_qkv, w_out, head_count):
    length, width = rows.shape
    rows_f = rows.astype(jnp.float32)
    normed = norm_scale(rows_f, gain).astype(jnp.bfloat16)
    qkv = jnp.dot(normed, w_qkv, preferred_element_type=jnp.float32).astype(jnp.bfloat16)
    positions = jnp.arange(length, dtype=jnp.int32)
    later = positions > done
    allowed = (positions[:, None] >= positions[None, :]) & (later[:, None] == later[None, :])
    mixed = attend(qkv, allowed, head_count).astype(jnp.bfloat16)
    added = jnp.dot(mixed, w_out, preferred_element_type=jnp.float32)
    return (rows_f + added).astype(jnp.bfloat16)


def left_product(left, right):
    return lax.dot_general(
        left, right, (((0,), (0,)), ((), ())), preferred_element_type=jnp.float32
    )


def agent_step(lifted, alive_rows, target_rows, gain, w_qk, z, w_value, head_count):
    agent_count, step_count, width = lifted.shape
    size = width // head_count
    lifted_f = lifted.astype(jnp.float32)
    normed_f, norm_pull = jax.vjp(lambda rows: norm_scale(rows, gain), lifted_f)
    normed = normed_f.astype(jnp.bfloat16).reshape(-1, width)
    qk = jnp.dot(normed, w_qk, preferred_element_type=jnp.float32).astype(jnp.bfloat16)
    qk = qk.reshape(agent_count, step_count, 2, head_count, size)
    q, k = qk[:, :, 0], qk[:, :, 1]
    s = jnp.dot(normed.astype(jnp.float32), z, precision=HI)
    s = s.reshape(agent_count, step_count, head_count).transpose(1, 2, 0)
    living = alive_rows.T == 1
    allowed = living[:, None, :] | jnp.eye(agent_count, dtype=bool)[None]
    scores = jnp.einsum("qbhe,kbhe->bhqk", q, k, preferred_element_type=jnp.float32)
    scores = jnp.where(allowed[:, None], scores / math.sqrt(size), -1e30)
    weights = jnp.exp(scores - jnp.max(scores, axis=-1, keepdims=True))
    probs = weights / jnp.sum(weights, axis=-1, keepdims=True)
    pv = jnp.sum(probs * s[:, :, None, :], axis=-1)
    predicted = jnp.sum(lifted_f * w_value, axis=-1) + jnp.sum(pv, axis=1).T
    err = 32.0 * alive_rows.astype(jnp.float32) * (predicted - target_rows)
    weighted = probs * err.T[:, None, :, None]
    t = jnp.sum(weighted, axis=2)
    ds = weighted * (s[:, :, None, :] - pv[..., None]) * (1.0 / math.sqrt(size))
    ds = ds.astype(jnp.bfloat16)
    dq = jnp.einsum("bhqk,kbhe->qbhe", ds, k, preferred_element_type=jnp.float32)
    dk = jnp.einsum("bhqk,qbhe->kbhe", ds, q, preferred_element_type=jnp.float32)
    dqk = jnp.stack([dq, dk], axis=2).astype(jnp.bfloat16).reshape(-1, 2 * width)
    t = t.transpose(2, 0, 1).reshape(-1, head_count)
    grad_normed = jnp.dot(dqk, w_qk.T, preferred_element_type=jnp.float32)
    grad_normed = grad_normed + jnp.dot(t, z.T, precision=HI)
    grad_top = err[..., None] * w_value
    grad_lifted = grad_top + norm_pull(grad_normed.reshape(agent_count, step_count, width))[0]
    return (predicted, grad_lifted.astype(jnp.bfloat16), normed, dqk, t)


def per_device(
    hidden, done_step, alive, targets, gain_t, w_qkv_t, w_out_t, gain_a, w_qkv_a, w_out_a, w_value
):
    width = hidden.shape[-1]
    size = width // HEADS
    local_rows = hidden[0, 0]
    done = done_step[0, 0]
    v = lax.all_gather(
        jnp.sum(w_out_a.astype(jnp.float32) * w_value, axis=1), "tm", axis=0, tiled=True
    )
    w_v = w_qkv_a[:, 2 * width :].astype(jnp.float32)
    z = jnp.sum((w_v * v).reshape(-1, HEADS, size), axis=-1)
    z = lax.all_gather(z, "tm", axis=0, tiled=True)
    w_qk = lax.all_gather(w_qkv_a[:, : 2 * width], "tm", axis=0, tiled=True)
    first, pull = jax.vjp(
        lambda rows: temporal_block(rows, done, gain_t, w_qkv_t, w_out_t, HEADS), local_rows
    )
    lifted = lax.all_to_all(first[None], "tm", split_axis=1, concat_axis=0, tiled=True)
    predicted, grad_lifted, normed, dqk, t = agent_step(
        lifted, alive[0], targets[0], gain_a, w_qk, z, w_value, HEADS
    )
    returned = lax.all_to_all(grad_lifted, "tm", split_axis=0, concat_axis=1, tiled=True)
    terms = left_product(normed, dqk).astype(jnp.bfloat16)
    u_terms = lax.dot_general(
        normed.astype(jnp.float32), t, (((0,), (0,)), ((), ())), precision=HI
    )
    summed = lax.psum_scatter(terms, "tm", scatter_dimension=0, tiled=True)
    qk_grad = lax.psum(summed, "env").astype(jnp.float32)
    u_mine = lax.psum(u_terms, ("env", "tm"))
    u_mine = lax.dynamic_slice_in_dim(
        u_mine, lax.axis_index("tm") * w_v.shape[0], w_v.shape[0], 0
    )
    u_wide = jnp.repeat(u_mine, size, axis=1)
    v_grad = u_wide * v
    mixed_err = lax.psum(jnp.sum(u_wide * w_v, axis=0), "tm")
    mixed_err = lax.dynamic_slice_in_dim(
        mixed_err, lax.axis_index("tm") * w_out_a.shape[0], w_out_a.shape[0], 0
    )
    out_grad = mixed_err[:, None] * w_value
    qkv_grad = jnp.concatenate([qk_grad, v_grad], axis=1)
    input_grad = pull(returned[0])[0]
    return (predicted[None], input_grad[None, None], qkv_grad, out_grad)


def solution(mesh):
    in_specs = (
        P("env", "tm", None, None),
        P("env", "tm"),
        P("env", None, "tm"),
        P("env", None, "tm"),
        P(),
        P(),
        P(),
        P(),
        P("tm", None),
        P("tm", None),
        P(),
    )
    out_specs = (P("env", None, "tm"), P("env", "tm", None, None), P("tm", None), P("tm", None))
    return jax.shard_map(
        per_device, mesh=mesh, in_specs=in_specs, out_specs=out_specs, check_vma=False
    )
```

time: 755 us -> 858 us (1.14)
  blocking collectives: 0 us -> 593 us
  waiting for transfers between devices: 592 us -> 128 us
  local copies, waits for them, and re-layouts: 42.7 us -> 30.5 us
    psum x0 -> x2, blocking collectives: none -> 288 us  [the longest x1 156 us: per_device(): mixed_err = lax.psum(jnp.sum(u_wide * w_v, axis=0), 'tm')]
    reduce_scatter x1, waiting for transfers between devices: 309 us -> 45.1 us  [per_device(): summed = lax.psum_scatter(terms, 'tm', scatter_dimension=0, tiled=True)]
    all_gather x2 -> x1, waiting for transfers between devices: 165 us -> 0.01 us  [per_device(): w_qk = lax.all_gather(w_qkv_a[:, :2 * width], 'tm', axis=0, tiled=True)]
    unnamed x0 -> x1, blocking collectives: none -> 157 us
    all_gather x0 -> x1, blocking collectives: none -> 148 us  [per_device(): z = lax.all_gather(z, 'tm', axis=0, tiled=True)]
    all_to_all x1, waiting for transfers between devices: 19.2 us -> 0.01 us  [per_device(): lax.all_to_all(grad_lifted, 'tm', split_axis=0, concat_axis=1, tiled=True)]
    all_to_all x1, waiting for transfers between devices: 16.4 us -> 0.01 us  [per_device(): lax.all_to_all(first[None], 'tm', split_axis=1, concat_axis=0, tiled=True)]
    dot_general x20 -> x17, matrix products: 36.7 us -> 37.2 us  [the longest x2 7.74 us: temporal_block(): jnp.dot(normed, w_qkv, preferred_element_type=jnp.float32)]
  transfers between devices with their start and end apart: 6 -> 5, of which waited for: 6 -> 2; matrix products, arithmetic and copies ran while one was open for 11% -> 8% of each run, Pallas kernels for 0% -> 0%
where the time goes in v1:
time: 858 us; the launch traced here: 857 us
  blocking collectives  593 us (69%)
  waiting for transfers between devices  128 us (15%)
  matrix products  45.3 us (5%)
  local copies, waits for them, and re-layouts  30.5 us (4%)
  other arithmetic  24.6 us (3%)
  starting transfers between devices  20.1 us (2%)
  between operations  15.7 us (2%)
    unnamed x1, blocking collectives  157 us
    psum x1, blocking collectives, per_device(): mixed_err = lax.psum(jnp.sum(u_wide * w_v, axis=0), 'tm')  156 us
    all_gather x1, blocking collectives, per_device(): z = lax.all_gather(z, 'tm', axis=0, tiled=True)  148 us
    psum x1, blocking collectives, per_device(): u_mine = lax.psum(u_terms, ('env', 'tm'))  132 us
    psum x1, waiting for transfers between devices, per_device(): qk_grad = lax.psum(summed, 'env').astype(jnp.float32)  82.4 us
    reduce_scatter x1, waiting for transfers between devices, per_device(): summed = lax.psum_scatter(terms, 'tm', scatter_dimension=0, tiled=True)  45.1 us
  transfers between devices with their start and end apart: 5, of which 2 were waited for; matrix products, arithmetic and copies ran while one was open for 8% of the time, Pallas kernels for 0%

profile of v1, /device:TPU:1, one launch (start us, length us, event | category | flops | bytes accessed | tf_op | source)
XLA Modules:
  0.0 856.8 jit_solution(7488116643575696525)
XLA Ops:
  7.2 1.6 slice.24
  9.5 1.2 fusion.49
  11.3 4.9 convolution_convert_fusion
  16.1 1.1 slice_bitcast_fusion
  17.2 1.4 copy.98
  18.7 2.2 copy.97
  21.0 1.6 fusion.114
  24.0 1.0 copy-done.3
  27.5 4.5 reduce.4
  32.0 2.2 reshape.279
  34.2 15.1 %all-to-all-start = ((bf16[64,2,2048]{2,1,0:T(2,128)(2,1)}), bf16[64,2,2048]{2,1,0:T(2,128)(2,1)S(1)}, u32[]{:S(2)}, u32[]{:S(2)}) async-start(bf16[64,2,2048]{2,1,0:T(2,128)(2,1)} %reshape.279), calls=%async_computation | async-start | bytes 1048576 | tf_op jit(solution)/shard_map/all_to_all | solution.py:103
  51.0 156.9 %all-reduce.3 = f32[1024]{0:T(1024)S(1)} all-reduce(f32[1024]{0:T(1024)S(1)} %dynamic-update-slice), channel_id=1, replica_groups=mesh['env'=4,'tm'=64] {'tm'}, use_global_device_ids=true, to_apply=%add.3 | all-reduce | flops 1024 | bytes 8192
  208.9 148.0 %all-gather = f32[64,16,8]{1,2,0:T(8,128)S(1)} all-gather(f32[1,16,8]{1,2,0:T(8,128)S(1)} %bitcast.169), channel_id=1, replica_groups=mesh['env'=4,'tm'=64] {'tm'}, dimensions={0}, use_global_device_ids=true | all-gather | bytes 33280 | tf_op jit(solution)/shard_map/all_gather | solution.py:98
  357.9 1.8 reshape.280
  359.7 1.6 fusion.39
  362.2 1.3 reshape.268
  363.5 1.5 multiply_convert_fusion
  365.8 1.3 convolution_bitcast_fusion.3
  367.1 3.5 fusion.16
  370.9 1.0 fusion.113
  371.9 3.5 multiply_reduce_fusion.2
  375.4 1.3 fusion.95
  376.7 3.3 convolution_bitcast_fusion
  380.0 3.4 convolution_bitcast_fusion.1
  383.5 1.3 maximum_convert_fusion
  384.8 1.7 copy.78
  386.4 2.3 convert_element_type.173
  388.7 4.6 convolution_convert_fusion.1
  394.1 1.6 multiply_reduce_fusion
  395.8 3.8 fusion.115
  399.6 2.1 fusion.40
  401.8 2.6 reshape.260
  404.4 2.8 fusion.47
  407.2 4.9 all-to-all-start.1
  412.1 1.5 convolution_bitcast_fusion.2
  413.6 132.2 %psum.22 = f32[1024,8]{0,1:T(8,128)S(1)} all-reduce(f32[1024,8]{0,1:T(8,128)S(1)} %convolution_bitcast_fusion.2), channel_id=1, replica_groups=mesh['env'=4,'tm'=64] {'env','tm'}, use_global_device_ids=true, to_apply=%region_19.20 | all-reduce | flops 8192 | bytes 65536 | tf_op jit(solution)/shard_map/psum | solution.py:114
  546.8 156.0 %psum.23 = f32[1024]{0:T(1024)S(1)} all-reduce(f32[1024]{0:T(1024)S(1)} %get-tuple-element.19), channel_id=1, replica_groups=mesh['env'=4,'tm'=64] {'tm'}, use_global_device_ids=true, to_apply=%region_21.22 | all-reduce | flops 1024 | bytes 8192 | tf_op jit(solution)/shard_map/psum | solution.py:120
  703.6 0.9 squeeze.21
  704.6 2.6 convolution_convert_fusion.5
  707.2 1.2 copy.94
  708.5 2.3 fusion.6
  710.9 1.0 convert_reduce_fusion
  712.6 1.2 fusion.25
  713.8 1.2 fusion.24
  716.0 2.9 fusion.52
  718.9 45.1 %reduce-scatter.2.cloned.1.call-done = bf16[16,2048]{1,0:T(8,128)(2,1)} async-done(((bf16[1024,2048]{1,0:T(8,128)(2,1)}), bf16[16,2048]{1,0:T(8,128)(2,1)}) %reduce-scatter.2.cloned.1.call-update) | async-done | bytes 65552 | tf_op jit(solution)/shard_map/reduce_scatter | solution.py:112
  764.1 2.3 fusion.67
  766.4 82.4 %all-reduce.6.cloned.1.call-done = bf16[16,2048]{1,0:T(8,128)(2,1)} async-done(((bf16[16,2048]{1,0:T(8,128)(2,1)}), bf16[16,2048]{1,0:T(8,128)(2,1)}) %all-reduce.6.cloned.1.call-update) | async-done | bytes 65552 | tf_op jit(solution)/shard_map/psum | solution.py:113
  (123 shorter events, 15.4 us)
Async XLA Ops:
  7.2 18.2 %copy-start = (bf16[1024,1024]{1,0:T(8,128)(2,1)S(1)}, bf16[1024,1024]{1,0:T(8,128)(2,1)}, u32[]{:S(2)}) copy-start(bf16[1024,1024]{1,0:T(8,128)(2,1)} %param.17) | copy-start | bytes 6291460
  7.2 359.9 %all-gather.3.cloned.1.call-start = ((), (), s32[]{:S(2)}) async-start(), calls=%async_computation.3 | async-start | bytes 4259840 | tf_op jit(solution)/shard_map/all_gather | solution.py:99
  10.7 0.5 copy-start.25
  11.3 4.9 copy-start.28
  17.2 6.8 copy-start.9
  18.7 3.9 copy-start.11
  22.6 1.4 copy-start.1
  22.9 2.4 copy-start.16
  22.9 2.4 copy-start.7
  24.0 1.0 copy-start.3
  26.9 22.4 %copy-start.31 = (u32[256]{0:T(256)S(1)}, u32[256]{0:T(256)}, u32[]{:S(2)}) copy-start(u32[256]{0:T(256)} %constant.61) | copy-start | bytes 3076
  26.9 23.7 %copy-start.18 = (f32[1024]{0:T(1024)S(1)}, f32[1024]{0:T(1024)}, u32[]{:S(2)}) copy-start(f32[1024]{0:T(1024)} %param.21) | copy-start | bytes 12292
  27.0 23.7 %copy-start.21 = (bf16[16,1024]{1,0:T(8,128)(2,1)S(1)}, bf16[16,1024]{1,0:T(8,128)(2,1)}, u32[]{:S(2)}) copy-start(bf16[16,1024]{1,0:T(8,128)(2,1)} %param.20) | copy-start | bytes 98308
  32.0 325.1 %copy-start.27 = (s32[1,64,4]{1,2,0:T(4,128)S(1)}, s32[1,64,4]{1,2,0:T(4,128)}, u32[]{:S(2)}) copy-start(s32[1,64,4]{1,2,0:T(4,128)} %param.13) | copy-start | bytes 3076
  34.2 323.7 %all-to-all-start = ((bf16[64,2,2048]{2,1,0:T(2,128)(2,1)}), bf16[64,2,2048]{2,1,0:T(2,128)(2,1)S(1)}, u32[]{:S(2)}, u32[]{:S(2)}) async-start(bf16[64,2,2048]{2,1,0:T(2,128)(2,1)} %reshape.279), calls=%async_computation | async-start | bytes 1048576 | tf_op jit(solution)/shard_map/all_to_all | solution.py:103
  49.3 714.7 %reduce-scatter.2.cloned.1.call-start = ((), (), s32[]{:S(2)}) async-start(), calls=%async_computation.4 | async-start | bytes 4259840 | tf_op jit(solution)/shard_map/reduce_scatter | solution.py:112
  207.9 149.2 %copy-start.19 = (f32[1024]{0:T(1024)}, f32[1024]{0:T(1024)S(1)}, u32[]{:S(2)}) copy-start(f32[1024]{0:T(1024)S(1)} %all-reduce.3) | copy-start | bytes 12292
  357.9 5.6 copy-start.15
  361.3 9.4 %copy-start.23 = (f32[256]{0:T(256)}, f32[256]{0:T(256)S(1)}, u32[]{:S(2)}) copy-start(f32[256]{0:T(256)S(1)} %get-tuple-element.24) | copy-start | bytes 3076
  365.0 0.8 copy-start.6
  384.8 4.0 copy-start.24
  393.3 0.7 copy-start.22
  401.7 2.7 copy-start.5
  404.4 7.7 copy-start.17
  404.4 141.6 %copy-start.20 = (f32[1024]{0:T(1024)S(1)}, f32[1024]{0:T(1024)}, u32[]{:S(2)}) copy-start(f32[1024]{0:T(1024)} %copy-done.19) | copy-start | bytes 12292
  407.2 296.4 %all-to-all-start.1 = ((bf16[64,4,1024]{2,1,0:T(4,128)(2,1)}), bf16[64,4,1024]{2,1,0:T(4,128)(2,1)S(1)}, u32[]{:S(2)}, u32[]{:S(2)}) async-start(bf16[64,4,1024]{2,1,0:T(4,128)(2,1)} %fusion.47), calls=%async_computation.1 | async-start | bytes 1048576 | tf_op jit(solution)/shard_map/all_to_all | solution.py:107
  412.0 436.7 %all-reduce.6.cloned.1.call-start = ((), (), s32[]{:S(2)}) async-start(), calls=%async_computation.5 | async-start | bytes 131072 | tf_op jit(solution)/shard_map/psum | solution.py:113
  704.6 3.9 copy-start.10
  708.5 2.4 copy-start.2
  710.8 1.2 copy-start.4
  710.8 1.7 copy-start.12
  712.5 1.2 copy-start.13
  712.5 2.4 slice-start
  713.8 1.5 copy-start.8
  713.8 2.2 slice-start.1
  713.8 2.2 copy-start.30
  716.0 2.9 copy-start.26
  716.0 48.0 %copy-start.14 = (bf16[256,1024]{1,0:T(8,128)(2,1)S(1)}, bf16[256,1024]{1,0:T(8,128)(2,1)}, u32[]{:S(2)}) copy-start(bf16[256,1024]{1,0:T(8,128)(2,1)} %squeeze.21) | copy-start | bytes 1572868
  716.0 48.0 %copy-start.29 = (f32[256]{0:T(256)S(1)}, f32[256]{0:T(256)}, u32[]{:S(2)}) copy-start(f32[256]{0:T(256)} %copy-done.28) | copy-start | bytes 3076
Sparse Core Ops, SparseCore 0:
  12.1 128.8 all-gather.2
  393.4 370.5 reduce-scatter.1
  766.8 81.8 all-reduce.5

commit v2 on v0

v2 whole, which is shorter than its diff:
```python
import math

import jax
import jax.numpy as jnp
from jax import lax
from jax.experimental import pallas as pl
from jax.experimental.pallas import tpu as pltpu
from jax.sharding import PartitionSpec as P

F32, BF16 = jnp.float32, jnp.bfloat16
HEADS, D, STEPS, AGENTS = 8, 1024, 256, 64
HD = D // HEADS
SCALE = 1.0 / math.sqrt(HD)
CUT = 512
WIDE = D + 128
NEG = -1e30


def dot(a, b, ca, cb):
    return lax.dot_general(a, b, (((ca,), (cb,)), ((), ())), preferred_element_type=F32)


def nn(a, b):
    return dot(a, b, 1, 0)


def nt(a, b):
    return dot(a, b, 1, 1)


def tn(a, b):
    return dot(a, b, 0, 0)


def iota(shape, axis):
    return lax.broadcasted_iota(jnp.int32, shape, axis)


def split(x):
    high = x.astype(BF16)
    return high, (x - high.astype(F32)).astype(BF16)


def pick(condition):
    return jnp.where(condition, 1.0, 0.0).astype(BF16)


def step_to_block(flip):
    i, c = iota((256, 256), 1 if flip else 0), iota((256, 256), 0 if flip else 1)
    return pick(((i // 4) % 4 == c // 64) & (c % 64 == (i // 16) * 4 + i % 4))


def block_to_agent(flip):
    i, c = iota((256, 256), 1 if flip else 0), iota((256, 256), 0 if flip else 1)
    return pick((i % 16 == c // 16) & (i // 16 == c % 16))


def kernel(
    hidden_h, done_v, rows_v, gain_t_v, wqkv_h, wout_h, gain_a_v, wqkva_v, wouta_v, wval_v,
    values_o, igrad_o, qkvg_o, outg_o,
    hid, wqkv, wout, norm_t, qkv, prob_t, mixed, stage1, a1, r1, xr,
    w2, vb, zb, ub, z128, na, nat, qk, prob_a, dqk, trow, gnorm, stage2, a2, r2, gh,
    tb, rx, cws, cwr, ccs, ccr, sa, ya, yb, sb, zbuf, fx, xbuf, fin, lbuf, cbuf, urow,
    lsem, gs, gr, as1, ar1, as2, ar2, vs, vr, zs, zr, us, ur, rs, rr, own_sem,
):
    me, env = lax.axis_index("tm"), lax.axis_index("env")
    core = env % 2
    xh, z, y = me // 32, (me // 4) % 8, me % 4
    core_id = {"env": env + 1 - 2 * core}
    lo_id = {"env": (env + 2) % 4}

    def tm_at(xh_, z_, y_):
        return {"tm": xh_ * 32 + z_ * 4 + y_}

    x_id = tm_at(1 - xh, z, y)

    def send(src, dst, sems, k, where):
        copy = pltpu.make_async_remote_copy(
            src_ref=src, dst_ref=dst, send_sem=sems[0].at[k], recv_sem=sems[1].at[k],
            device_id=where, device_id_type=pl.DeviceIdType.MESH,
        )
        copy.start()
        return copy

    def spread(body):
        def step(i, carry):
            body(lax.rem(me + i, 64))
            return carry
        lax.fori_loop(1, 64, step, 0)

    loads = [pltpu.make_async_copy(hidden_h, hid, lsem.at[0])]
    for j in range(6):
        at = (slice(None), slice(512 * j, 512 * j + 512))
        loads.append(pltpu.make_async_copy(wqkv_h.at[at], wqkv.at[at], lsem.at[1 + j]))
    loads.append(pltpu.make_async_copy(wout_h, wout, lsem.at[7]))
    for load in loads:
        load.start()

    barrier = pltpu.get_barrier_semaphore()

    def greet(peer):
        pl.semaphore_signal(
            barrier, inc=1, device_id={"tm": peer}, device_id_type=pl.DeviceIdType.MESH
        )

    spread(greet)
    for i in (1, 2, 3):
        pl.semaphore_signal(
            barrier, inc=1, device_id={"env": (env + i) % 4}, device_id_type=pl.DeviceIdType.MESH
        )

    w_value = wval_v[...]
    lane_off = (me % 8) * 16
    spot = iota((16, 128), 1) == iota((16, 128), 0) + lane_off

    def to_lanes(column):
        return jnp.sum(jnp.where(spot, column, 0.0), axis=0, keepdims=True)

    own_rows = pl.ds(pl.multiple_of(y * 16, 16), 16)
    mine = wqkva_v[:, :D]
    other = wqkva_v[:, D : 2 * D]
    w2[core, xh, z, own_rows, :] = jnp.where(core == 0, mine, other)
    v_part = jnp.sum(wouta_v[...].astype(F32) * w_value, axis=1, keepdims=True)
    vb[me] = to_lanes(v_part)

    pl.semaphore_wait(barrier, 66)

    G, V, Z, U, R = (gs, gr), (vs, vr), (zs, zr), (us, ur), (rs, rr)
    a_cols, b_cols = pl.ds(0, 512), pl.ds(512, 512)

    def put_v(peer):
        send(vb.at[me], vb.at[me], V, 0, {"tm": peer})

    def put_z(peer):
        send(zb.at[me], zb.at[me], Z, 0, {"tm": peer})

    def put_u(peer):
        row = peer // 8
        send(urow.at[row], ub.at[me], U, 0, {"tm": peer})

    def all_of(ref, sems, n):
        return pltpu.make_async_remote_copy(
            src_ref=ref.at[pl.ds(0, n)], dst_ref=ref.at[pl.ds(0, n)], send_sem=sems[0].at[0],
            recv_sem=sems[1].at[0], device_id=x_id, device_id_type=pl.DeviceIdType.MESH,
        )

    def piece(xs, zs_, rows, cols):
        return w2.at[core, xs, zs_, rows, cols]

    whole = pl.ds(0, 64)
    both = pl.ds(0, 2)
    every = pl.ds(0, 8)
    live = {}

    def relay(name, k, ref, where):
        live[name] = send(ref, ref, G, k, where)

    def g_x():
        relay("x", 0, piece(xh, z, own_rows, pl.ds(0, D)), x_id)

    def g_yz():
        live["x"].wait()
        for i in (1, 2, 3):
            relay(("ya", i), i, piece(both, z, own_rows, a_cols), tm_at(xh, z, (y + i) % 4))
        for i in range(1, 8):
            relay(("zb", i), 3 + i, piece(both, z, own_rows, b_cols), tm_at(xh, (z + i) % 8, y))

    def ring(k):
        if k <= 4:
            at = (z + 9 - k) % 8
            relay(("cw", k), 10 + k, piece(both, at, whole, a_cols), tm_at(xh, (z + 1) % 8, y))
        if k <= 3:
            at = (z + k - 1) % 8
            relay(("cc", k), 14 + k, piece(both, at, whole, a_cols), tm_at(xh, (z + 7) % 8, y))

    def to_core(k, ref):
        relay(("core", k), 21 + k, ref, core_id)

    def g_ring1():
        for i in (1, 2, 3):
            live[("ya", i)].wait()
        ring(1)
        to_core(0, piece(both, z, whole, a_cols))

    def g_b():
        for i in range(1, 8):
            live[("zb", i)].wait()
        for i in (1, 2, 3):
            relay(
                ("yb", i), 17 + i, piece(both, every, own_rows, b_cols), tm_at(xh, z, (y + i) % 4)
            )
        to_core(1, piece(both, every, own_rows, b_cols))

    def g_ring(k):
        live[("cw", k)].wait()
        if k <= 3:
            live[("cc", k)].wait()
        if k < 4:
            ring(k + 1)
        to_core(2 * k, piece(both, (z + 8 - k) % 8, whole, a_cols))
        if k <= 3:
            to_core(2 * k + 1, piece(both, (z + k) % 8, whole, a_cols))

    def g_b_end():
        for i in (1, 2, 3):
            live[("yb", i)].wait()
            rows = pl.ds(pl.multiple_of(((y + 4 - i) % 4) * 16, 16), 16)
            to_core(8 + i, piece(both, every, rows, b_cols))

    def v_ready():
        all_of(vb, V, 63).wait()

    def make_z():
        v_ready()
        v8 = jnp.sum(vb[...].reshape(8, 8, 128), axis=1)
        rows = []
        for h in range(HEADS):
            w_v = wqkva_v[:, 2 * D + h * HD : 2 * D + (h + 1) * HD].astype(F32)
            col = jnp.sum(w_v * v8[h : h + 1, :], axis=1, keepdims=True)
            rows.append(to_lanes(col))
        zb[me] = jnp.concatenate(rows, axis=0)
        spread(put_z)
        return v8

    g_x()
    spread(put_v)

    loads[0].wait()
    x = hid[...].astype(F32)
    inv_t = lax.rsqrt(jnp.mean(x * x, axis=1, keepdims=True) + 1e-6)
    norm_t[...] = (x * inv_t * gain_t_v[...]).astype(BF16)
    for j in range(6):
        loads[1 + j].wait()
        at = slice(512 * j, 512 * j + 512)
        qkv[:, at] = nn(norm_t[...], wqkv[:, at]).astype(BF16)
        if j == 0:
            g_yz()
        if j == 2:
            g_ring1()
        if j == 4:
            g_b()
    done = done_v[...]
    ri, ci = iota((STEPS, STEPS), 0), iota((STEPS, STEPS), 1)
    allowed_t = (ri >= ci) & ((ri > done) == (ci > done))
    v8 = None
    for h in range(HEADS):
        at = slice(h * HD, (h + 1) * HD)
        s = nt(qkv[:, at], qkv[:, D + h * HD : D + (h + 1) * HD]) * SCALE
        s = jnp.where(allowed_t, s, NEG)
        e = jnp.exp(s - jnp.max(s, axis=1, keepdims=True))
        p = (e / jnp.sum(e, axis=1, keepdims=True)).astype(BF16)
        prob_t[h] = p
        mixed[:, at] = nn(p, qkv[:, 2 * D + h * HD : 2 * D + (h + 1) * HD]).astype(BF16)
        if h == 1:
            v8 = make_z()
        if h == 2:
            g_ring(1)
        if h == 5:
            g_ring(2)
    loads[7].wait()
    turn = step_to_block(False)
    for q in range(4):
        at = slice(256 * q, 256 * q + 256)
        h1 = (hid[:, at].astype(F32) + nn(mixed[...], wout[:, at])).astype(BF16)
        for j in range(4):
            stage1[j, q * 64 : q * 64 + 64, :] = h1[j * 64 : j * 64 + 64, :]
    for j in range(4):
        a1[j * 256 : j * 256 + 256, :] = nn(turn, stage1[j]).astype(BF16)

    def block(peer):
        return pl.ds(pl.multiple_of(peer * 16, 16), 16)

    def put_1(peer):
        send(a1.at[block(peer)], r1.at[block(me)], (as1, ar1), 0, {"tm": peer})

    spread(put_1)
    r1[block(me), :] = a1[block(me), :]
    g_ring(3)
    g_ring(4)
    g_b_end()

    all_of(zb, Z, 63).wait()
    zt = jnp.concatenate(
        [jnp.sum(zb[8 * j : 8 * j + 8], axis=0) for j in range(8)], axis=1
    )
    z_hi, z_lo = split(zt)
    z128[...] = jnp.zeros((128, D), BF16)
    z128[0:16, :] = jnp.concatenate([z_hi, z_hi], axis=0)
    z128[16:32, :] = jnp.concatenate([z_lo, jnp.zeros_like(z_lo)], axis=0)

    def wait_all(src, dst, sems):
        pltpu.make_async_remote_copy(
            src_ref=src.at[pl.ds(0, 1008)], dst_ref=dst.at[pl.ds(0, 1008)], send_sem=sems[0].at[0],
            recv_sem=sems[1].at[0], device_id=x_id, device_id_type=pl.DeviceIdType.MESH,
        ).wait()

    wait_all(a1, r1, (as1, ar1))

    unturn = block_to_agent(False)
    for j in range(4):
        got = nn(unturn, r1[j * 256 : j * 256 + 256, :]).astype(BF16)
        for q in range(4):
            for s in range(4):
                i = (q * 4 + s) * 16
                xr[s * 64 + j * 16 : s * 64 + j * 16 + 16, q * 256 : q * 256 + 256] = got[
                    i : i + 16, :
                ]
    xa = xr[...].astype(F32)
    inv_a = lax.rsqrt(jnp.mean(xa * xa, axis=1, keepdims=True) + 1e-6)
    h1_value = jnp.sum(xa * w_value, axis=1, keepdims=True)
    normed = xa * inv_a * gain_a_v[...]
    na[...] = normed.astype(BF16)
    for j in range(4):
        nat[j * 256 : j * 256 + 256, :] = normed[:, j * 256 : j * 256 + 256].T.astype(BF16)
    for k in range(12):
        live[("core", k)].wait()
    for c in range(2):
        for i in range(2):
            w = w2[c, :, :, :, 512 * i : 512 * i + 512].reshape(D, 512)
            at = c * D + 512 * i
            qk[:, at : at + 512] = nn(na[...], w).astype(BF16)
    s_rows = nt(z128[0:32, :], na[...])
    s_rows = s_rows[0:8] + s_rows[16:24]
    diag = ri == ci
    alive_row, target_row = rows_v[0:1, :], rows_v[1:2, :]

    def to_column(row):
        return jnp.sum(jnp.where(diag, row, 0.0), axis=1, keepdims=True)

    alive_col, target_col = to_column(alive_row), to_column(target_row)
    half = iota((128, 128), 0), iota((128, 128), 1)
    same_step = (half[0] // 64) == (half[1] // 64)
    sums = []
    for p in range(2):
        rows = slice(128 * p, 128 * p + 128)
        seen = same_step & ((alive_row[:, rows] == 1.0) | (half[0] == half[1]))
        total = jnp.zeros((128, 1), F32)
        for h in range(HEADS):
            at = slice(h * HD, (h + 1) * HD)
            s = nt(qk[rows, at], qk[rows, D + h * HD : D + (h + 1) * HD]) * SCALE
            s = jnp.where(seen, s, NEG)
            e = jnp.exp(s - jnp.max(s, axis=1, keepdims=True))
            e = e / jnp.sum(e, axis=1, keepdims=True)
            prob_a[h, p] = e
            total = total + jnp.sum(e * s_rows[h : h + 1, rows], axis=1, keepdims=True)
        sums.append(total)
    predicted = h1_value + jnp.concatenate(sums, axis=0)
    err = 32.0 * alive_col * (predicted - target_col)
    values_o[...] = jnp.sum(jnp.where(diag, predicted, 0.0), axis=0, keepdims=True)
    for p in range(2):
        rows = slice(128 * p, 128 * p + 128)
        for h in range(HEADS):
            at, at_k = slice(h * HD, (h + 1) * HD), slice(D + h * HD, D + (h + 1) * HD)
            e = prob_a[h, p]
            s_row = s_rows[h : h + 1, rows]
            pv = jnp.sum(e * s_row, axis=1, keepdims=True)
            weighted = e * err[rows, :]
            trow[h : h + 1, rows] = jnp.sum(weighted, axis=0, keepdims=True)
            ds = weighted * (s_row - pv) * SCALE
            dqk[rows, at] = nn(ds.astype(BF16), qk[rows, at_k]).astype(BF16)
            dqk[rows, at_k] = nn(ds.T.astype(BF16), qk[rows, at]).astype(BF16)
    t_hi = trow[...].astype(BF16).astype(F32)
    t_lo = trow[...] - t_hi
    t_all = jnp.concatenate([t_hi, t_lo, t_hi, jnp.zeros((104, STEPS), F32)], axis=0)
    t_col = t_all.T.astype(BF16)
    for i in range(4):
        at = slice(256 * i, 256 * i + 256)
        part = nn(t_col, z128[:, at])
        for c in range(2):
            w = w2[c, i // 2, 4 * (i % 2) : 4 * (i % 2) + 4].reshape(256, D)
            part = part + nt(dqk[:, c * D : c * D + D], w)
        gnorm[:, at] = part * gain_a_v[:, at]
    gy = gnorm[...]
    xa = xr[...].astype(F32)
    pull = jnp.mean(xa * gy, axis=1, keepdims=True) * (inv_a * inv_a * inv_a)
    grad = (err * w_value + gy * inv_a - xa * pull).astype(BF16)
    turn = block_to_agent(True)
    for j in range(4):
        for q in range(4):
            for s in range(4):
                i = (q * 4 + s) * 16
                stage2[i : i + 16, j * 256 : j * 256 + 256] = grad[
                    s * 64 + j * 16 : s * 64 + j * 16 + 16, q * 256 : q * 256 + 256
                ]
    for j in range(4):
        a2[j * 256 : j * 256 + 256, :] = nn(turn, stage2[:, j * 256 : j * 256 + 256]).astype(BF16)

    def put_2(peer):
        send(a2.at[block(peer)], r2.at[block(me)], (as2, ar2), 0, {"tm": peer})

    spread(put_2)
    r2[block(me), :] = a2[block(me), :]

    u_term = nn(nat[...], t_col).astype(BF16).reshape(2, 8, 64, 128)
    for c in range(2):
        for i in range(2):
            at = slice(512 * i, 512 * i + 512)
            part = nn(nat[...], dqk[:, c * D + 512 * i : c * D + 512 * i + 512])
            tb[c, :, :, :, at] = part.astype(BF16).reshape(2, 8, 64, 512)
        tb[c, :, :, :, D:WIDE] = u_term
    to_other = send(tb.at[1 - core], rx, R, 0, core_id)

    wait_all(a2, r2, (as2, ar2))
    unturn = step_to_block(True)
    for j in range(4):
        got = nn(unturn, r2[j * 256 : j * 256 + 256, :]).astype(BF16)
        for q in range(4):
            gh[j * 64 : j * 64 + 64, q * 256 : q * 256 + 256] = got[q * 64 : q * 64 + 64, :]

    cut_a, cut_b = pl.ds(0, CUT), pl.ds(CUT, WIDE - CUT)

    def r_start():
        to_other.wait()
        for i in range(2):
            for j in range(8):
                rx[i, j] = rx[i, j] + tb[core, i, j]
        live["cw1"] = send(
            rx.at[both, (z + 4) % 8, whole, cut_a], cwr.at[0], R, 1, tm_at(xh, (z + 1) % 8, y)
        )
        live["cc1"] = send(
            rx.at[both, (z + 5) % 8, whole, cut_a], ccr.at[0], R, 5, tm_at(xh, (z + 7) % 8, y)
        )
        for i in (1, 2, 3):
            there = (y + i) % 4
            rows = pl.ds(pl.multiple_of(there * 16, 16), 16)
            live[("yb2", i)] = send(
                rx.at[both, every, rows, cut_b], yb.at[i - 1], R, 7 + i, tm_at(xh, z, there)
            )

    def r_ring(k):
        live[f"cw{k - 1}"].wait()
        cws[k - 2] = cwr[k - 2] + rx[:, (z + 5 - k) % 8, :, 0:CUT]
        live[f"cw{k}"] = send(cws.at[k - 2], cwr.at[k - 1], R, k, tm_at(xh, (z + 1) % 8, y))
        if k <= 3:
            live[f"cc{k - 1}"].wait()
            ccs[k - 2] = ccr[k - 2] + rx[:, (z + 4 + k) % 8, :, 0:CUT]
            live[f"cc{k}"] = send(ccs.at[k - 2], ccr.at[k - 1], R, 4 + k, tm_at(xh, (z + 7) % 8, y))

    def r_b():
        for i in (1, 2, 3):
            live[("yb2", i)].wait()
        for i in range(2):
            for j in range(8):
                total = rx[i, j, own_rows, CUT:WIDE].astype(F32)
                for k in range(3):
                    total = total + yb[k, i, j].astype(F32)
                sb[i, j] = total.astype(BF16)
        for i in range(1, 8):
            there = (z + i) % 8
            live[("zb2", i)] = send(
                sb.at[both, there], zbuf.at[i - 1], R, 10 + i, tm_at(xh, there, y)
            )

    def r_a_end():
        live["cw4"].wait()
        live["cc3"].wait()
        total = cwr[3].astype(F32) + ccr[2].astype(F32) + rx[:, z, :, 0:CUT].astype(F32)
        sa[...] = total.astype(BF16)
        for i in (1, 2, 3):
            there = (y + i) % 4
            rows = pl.ds(pl.multiple_of(there * 16, 16), 16)
            live[("ya2", i)] = send(
                sa.at[both, rows], ya.at[i - 1], R, 17 + i, tm_at(xh, z, there)
            )

    def r_x():
        for i in range(1, 8):
            live[("zb2", i)].wait()
        total = sb[:, z].astype(F32)
        for k in range(7):
            total = total + zbuf[k].astype(F32)
        fx[:, :, CUT:WIDE] = total
        for i in (1, 2, 3):
            live[("ya2", i)].wait()
        total = sa[:, own_rows, :].astype(F32)
        for k in range(3):
            total = total + ya[k].astype(F32)
        fx[:, :, 0:CUT] = total
        live["x2"] = send(fx.at[1 - xh], xbuf, R, 21, x_id)

    def r_lo():
        live["x2"].wait()
        fin[...] = fx[xh] + xbuf[...]
        live["lo"] = send(fin, lbuf, R, 22, lo_id)

    def r_core():
        live["lo"].wait()
        total = fin[...] + lbuf[...]
        cbuf[core] = total[:, 0:D]
        live["core2"] = send(cbuf.at[core], cbuf.at[core], R, 23, core_id)
        u = total[:, D : D + 8] + total[:, D + 8 : D + 16]
        wide = jnp.concatenate(
            [jnp.broadcast_to(u[:, h : h + 1], (16, HD)) for h in range(HEADS)], axis=1
        )
        v_wide = jnp.concatenate([v8[h : h + 1, :] for h in range(HEADS)], axis=1)
        qkvg_o[:, 2 * D : 3 * D] = wide * v_wide
        weighted = jnp.sum(wide * wqkva_v[:, 2 * D : 3 * D].astype(F32), axis=0, keepdims=True)
        for j in range(8):
            urow[j] = weighted[:, 128 * j : 128 * j + 128]
        ub[me] = urow[me // 8]
        spread(put_u)

    def r_end():
        live["core2"].wait()
        qkvg_o[:, 0:D] = cbuf[0]
        qkvg_o[:, D : 2 * D] = cbuf[1]
        all_of(ub, U, 63).wait()
        row = jnp.sum(ub[...].reshape(64, 128), axis=0, keepdims=True)
        column = jnp.sum(jnp.where(spot, row, 0.0), axis=1, keepdims=True)
        outg_o[...] = column * w_value

    r_start()
    after = {1: lambda: r_ring(2), 3: lambda: r_ring(3), 5: lambda: (r_ring(4), r_b()), 7: r_a_end}
    for h in range(HEADS):
        at = slice(h * HD, (h + 1) * HD)
        at_k, at_v = slice(D + h * HD, D + (h + 1) * HD), slice(2 * D + h * HD, 2 * D + (h + 1) * HD)
        gm = nt(gh[...], wout[at, :]).astype(BF16)
        p = prob_t[h]
        pf = p.astype(F32)
        dp = nt(gm, qkv[:, at_v])
        ds = (pf * (dp - jnp.sum(pf * dp, axis=1, keepdims=True)) * SCALE)
        q_h, k_h = qkv[:, at], qkv[:, at_k]
        qkv[:, at_v] = nn(pf.T.astype(BF16), gm).astype(BF16)
        qkv[:, at] = nn(ds.astype(BF16), k_h).astype(BF16)
        qkv[:, at_k] = nn(ds.T.astype(BF16), q_h).astype(BF16)
        if h in after:
            after[h]()
    after = {1: r_x, 2: r_lo, 3: r_core}
    for i in range(4):
        at = slice(256 * i, 256 * i + 256)
        gnorm[:, at] = nt(qkv[...], wqkv[at, :]) * gain_t_v[:, at]
        if i in after:
            after[i]()
    gy = gnorm[...]
    x = hid[...].astype(F32)
    inv_t = lax.rsqrt(jnp.mean(x * x, axis=1, keepdims=True) + 1e-6)
    pull = jnp.mean(x * gy, axis=1, keepdims=True) * (inv_t * inv_t * inv_t)
    igrad_o[...] = (gh[...].astype(F32) + gy * inv_t - x * pull).astype(BF16)
    r_end()


def per_device(
    hidden, done_step, alive, targets, gain_t, w_qkv_t, w_out_t, gain_a, w_qkv_a, w_out_a, w_value
):
    rows = jnp.stack([alive[0].astype(F32).T.reshape(-1), targets[0].T.reshape(-1)])
    vmem = pl.BlockSpec(memory_space=pltpu.VMEM)
    away = pl.BlockSpec(memory_space=pl.ANY)
    mem = pltpu.VMEM
    dma = pltpu.SemaphoreType.DMA
    scratch = [
        mem((STEPS, D), BF16), mem((D, 3 * D), BF16), mem((D, D), BF16), mem((STEPS, D), BF16),
        mem((STEPS, 3 * D), BF16), mem((HEADS, STEPS, STEPS), BF16), mem((STEPS, D), BF16),
        mem((4, 256, 256), BF16), mem((1024, 256), BF16), mem((1024, 256), BF16),
        mem((STEPS, D), BF16),
        mem((2, 2, 8, 64, D), BF16), mem((64, 1, 128), F32), mem((64, 8, 128), F32),
        mem((64, 1, 128), F32), mem((128, D), BF16), mem((STEPS, D), BF16), mem((D, STEPS), BF16),
        mem((STEPS, 2 * D), BF16), mem((HEADS, 2, 128, 128), F32), mem((STEPS, 2 * D), BF16),
        mem((HEADS, STEPS), F32), mem((STEPS, D), F32), mem((256, 1024), BF16),
        mem((1024, 256), BF16), mem((1024, 256), BF16), mem((STEPS, D), BF16),
        mem((2, 2, 8, 64, WIDE), BF16), mem((2, 8, 64, WIDE), BF16), mem((3, 2, 64, CUT), BF16),
        mem((4, 2, 64, CUT), BF16), mem((2, 2, 64, CUT), BF16), mem((3, 2, 64, CUT), BF16),
        mem((2, 64, CUT), BF16), mem((3, 2, 16, CUT), BF16), mem((3, 2, 8, 16, WIDE - CUT), BF16),
        mem((2, 8, 16, WIDE - CUT), BF16), mem((7, 2, 16, WIDE - CUT), BF16),
        mem((2, 16, WIDE), F32), mem((16, WIDE), F32), mem((16, WIDE), F32), mem((16, WIDE), F32),
        mem((2, 16, D), F32), mem((8, 1, 128), F32),
        dma((8,)), dma((33,)), dma((33,)), dma((1,)), dma((1,)), dma((1,)), dma((1,)), dma((1,)),
        dma((1,)), dma((1,)), dma((1,)), dma((1,)), dma((1,)), dma((24,)), dma((24,)), dma((1,)),
    ]
    values, input_grad, qkv_grad, out_grad = pl.pallas_call(
        kernel,
        out_shape=(
            jax.ShapeDtypeStruct((1, STEPS), F32),
            jax.ShapeDtypeStruct((STEPS, D), BF16),
            jax.ShapeDtypeStruct((16, 3 * D), F32),
            jax.ShapeDtypeStruct((16, D), F32),
        ),
        in_specs=[away, vmem, vmem, vmem, away, away, vmem, vmem, vmem, vmem],
        out_specs=(vmem, vmem, vmem, vmem),
        scratch_shapes=scratch,
        compiler_params=pltpu.CompilerParams(
            collective_id=0, has_side_effects=True, vmem_limit_bytes=60 * 2**20
        ),
    )(
        hidden[0, 0], done_step, rows, gain_t[None], w_qkv_t, w_out_t, gain_a[None], w_qkv_a,
        w_out_a, w_value[None],
    )
    values = values.reshape(-1, AGENTS).T
    return values[None], input_grad[None, None], qkv_grad, out_grad


def solution(mesh):
    in_specs = (
        P("env", "tm", None, None),
        P("env", "tm"),
        P("env", None, "tm"),
        P("env", None, "tm"),
        P(),
        P(),
        P(),
        P(),
        P("tm", None),
        P("tm", None),
        P(),
    )
    out_specs = (P("env", None, "tm"), P("env", "tm", None, None), P("tm", None), P("tm", None))
    return jax.shard_map(
        per_device, mesh=mesh, in_specs=in_specs, out_specs=out_specs, check_vma=False
    )
```

time: 755 us -> 132 us (0.17)
  the two profiles are of different devices: /device:TPU:1 before, /device:TPU:8 now
where the time goes in v2:
time: 132 us; the launch traced here: 131 us
  Pallas kernels  120 us (91%)
  local copies, waits for them, and re-layouts  6.98 us (5%)
  other arithmetic  2.6 us (2%)
    pallas_call x1, Pallas kernels, per_device(): pl.pallas_call(kernel, out_shape=(jax.ShapeDtypeStruct((1, STEPS), F32),...  120 us
    unnamed x3, local copies, waits for them, and re-layouts  4.96 us

profile of v2, /device:TPU:8, one launch (start us, length us, event | category | flops | bytes accessed | tf_op | source)
XLA Modules:
  0.0 131.3 jit_solution(5193435797346366602)
XLA Ops:
  1.3 0.8 stack_reshape.7
  2.0 0.7 convert_bitcast_fusion
  2.7 0.1 stack_reshape.6
  2.8 0.6 pad_maximum_fusion.rows_v
  3.4 120.4 %shard_map.138 = (f32[1,256]{1,0:T(1,128)}, bf16[256,1024]{1,0:T(8,128)(2,1)}, f32[16,3072]{1,0:T(8,128)}, f32[16,1024]{1,0:T(8,128)}) custom-call(bf16[256,1024]{1,0:T(8,128)(2,1)} %bitcast.15, s32[1,1]{1,0:T(1,128)S(6)} %copy.18.done_v, f32[2,256]{1,0:T(2,128)} %pad_maximum_fusion.rows_v, f32[1,1024]{1,0:T(1,128)} %bitcast.17, bf16[1024,3072]{1,0:T(8,128)(2,1)} %wqkv_h.1, ...), custom_call_target="tpu_custom_call" | custom-call | tf_op jit(solution)/shard_map/pallas_call | solution.py:569
  123.8 0.5 broadcast.3
  124.3 1.3 %reduce.3 = f32[256]{0:T(256)S(1)} reduce(f32[1,256]{1,0:T(1,128)} %get-tuple-element.8, f32[]{:T(128)} %broadcast.3), dimensions={0}, to_apply=%get-tuple-element.8.reduce_sub_computation.3 | reduce | bytes 2052 | tf_op jit(solution)/shard_map/pallas_call | solution.py:569
  125.6 0.7 reshape.12
  126.3 1.9 %copy.19 = bf16[1,1,256,1024]{3,2,1,0:T(8,128)(2,1)} copy(bf16[1,1,256,1024]{3,2,1,0:T(8,128)(2,1)} %bitcast.16) | data formatting | bytes 1048576
  128.2 1.6 %copy.20 = f32[16,3072]{1,0:T(8,128)} copy(f32[16,3072]{1,0:T(8,128)} %get-tuple-element.18) | data formatting | bytes 393216
  129.8 1.5 %copy.21 = f32[16,1024]{1,0:T(8,128)} copy(f32[16,1024]{1,0:T(8,128)} %get-tuple-element.19) | data formatting | bytes 131072

commit v3 on v2

v3 whole, which is shorter than its diff:
```python
import math

import jax
import jax.numpy as jnp
from jax import lax
from jax.experimental import pallas as pl
from jax.experimental.pallas import tpu as pltpu
from jax.sharding import PartitionSpec as P

F32, BF16 = jnp.float32, jnp.bfloat16
HEADS, D, STEPS, AGENTS = 8, 1024, 256, 64
HD = D // HEADS
SCALE = 1.0 / math.sqrt(HD)
NEG = -1e30
BAR, V2_AT, G2_AT = 5, 3, 7


def dot(a, b, ca, cb):
    return lax.dot_general(a, b, (((ca,), (cb,)), ((), ())), preferred_element_type=F32)


def nn(a, b):
    return dot(a, b, 1, 0)


def nt(a, b):
    return dot(a, b, 1, 1)


def tn(a, b):
    return dot(a, b, 0, 0)


def iota(shape, axis):
    return lax.broadcasted_iota(jnp.int32, shape, axis)


def split(x):
    high = x.astype(BF16)
    return high, (x - high.astype(F32)).astype(BF16)


def pick(condition):
    return jnp.where(condition, 1.0, 0.0).astype(BF16)


def step_to_block(flip):
    i, c = iota((256, 256), 1 if flip else 0), iota((256, 256), 0 if flip else 1)
    return pick(((i // 4) % 4 == c // 64) & (c % 64 == (i // 16) * 4 + i % 4))


def block_to_agent(flip):
    i, c = iota((256, 256), 1 if flip else 0), iota((256, 256), 0 if flip else 1)
    return pick((i % 16 == c // 16) & (i // 16 == c % 16))


def kernel(
    hidden_h, done_v, rows_v, gain_t_v, wqkv_h, wout_h, gain_a_v, wqkva_v, wouta_v, wval_v,
    values_o, igrad_o, qkvg_o, outg_o,
    hid, wqkv, wout, norm_t, qkv, prob_t, mixed, stage1, a1, r1, xr,
    w2, vb1, vb2, zb1, zb2, z128, na, nat, qk, prob_a, dqk, dqr, trow, gnorm, stage2, a2, r2, gh,
    tb, p1y, p1x, s1, s2, p2x, p2y, s3, pz, eb, us1, uz, um, uxy, uf, ue, up, uq, uw, ux,
    lsem, gs, gr, as1, ar1, as2, ar2, ss, sr, rs, rr,
):
    me, env = lax.axis_index("tm"), lax.axis_index("env")
    core, xl = env % 2, env // 2
    xh, z, y = me // 32, (me // 4) % 8, me % 4
    x_at = xh * 2 + xl
    core_id = {"env": env + 1 - 2 * core}

    def tm_at(xh_, z_, y_):
        return {"tm": xh_ * 32 + z_ * 4 + y_}

    def x_of(i):
        to = (x_at + i) % 4
        return to // 2, to % 2

    def x_peer(i):
        to_h, to_l = x_of(i)
        return {"env": to_l * 2 + core, "tm": to_h * 32 + z * 4 + y}

    def y_peer(i):
        return tm_at(xh, z, (y + i) % 4)

    def z_peer(i):
        return tm_at(xh, (z + i) % 8, y)

    def xy_of(i):
        to = (xh * 4 + y + i) % 8
        return to // 4, to % 4

    def xy_peer(i):
        to_h, to_y = xy_of(i)
        return tm_at(to_h, z, to_y)

    def send(src, dst, sems, k, where):
        copy = pltpu.make_async_remote_copy(
            src_ref=src, dst_ref=dst, send_sem=sems[0].at[k], recv_sem=sems[1].at[k],
            device_id=where, device_id_type=pl.DeviceIdType.MESH,
        )
        copy.start()
        return copy

    def spread(body):
        def step(i, carry):
            body(lax.rem(me + i, 64))
            return carry
        lax.fori_loop(1, 64, step, 0)

    barrier = pltpu.get_barrier_semaphore()

    def greet(where):
        pl.semaphore_signal(
            barrier, inc=1, device_id=where, device_id_type=pl.DeviceIdType.MESH
        )

    for i in range(1, 8):
        greet(z_peer(i))
    for i in range(1, 8):
        greet(xy_peer(i))
    greet({"env": (env + 2) % 4, "tm": (1 - xh) * 32 + z * 4 + y})
    for i in (1, 2, 3):
        greet({"env": (env + i) % 4})

    loads = [pltpu.make_async_copy(hidden_h, hid, lsem.at[0])]
    for j in range(6):
        at = (slice(None), slice(512 * j, 512 * j + 512))
        loads.append(pltpu.make_async_copy(wqkv_h.at[at], wqkv.at[at], lsem.at[1 + j]))
    loads.append(pltpu.make_async_copy(wout_h, wout, lsem.at[7]))
    for load in loads:
        load.start()

    w_value = wval_v[...]
    lane_off = (me % 8) * 16
    spot = iota((16, 128), 1) == iota((16, 128), 0) + lane_off
    own_line = iota((8, 128), 0) == me // 8

    def to_lanes(column):
        return jnp.sum(jnp.where(spot, column, 0.0), axis=0, keepdims=True)

    def rows_of(y_):
        return pl.ds(pl.multiple_of(y_ * 16, 16), 16)

    own_rows = rows_of(y)
    for half in range(2):
        at = pl.multiple_of(core * D + half * 512 + xl * 256, 256)
        w2[core, half, xl, xh, z, own_rows, :] = wqkva_v[:, pl.ds(at, 256)]
    v_part = jnp.sum(wouta_v[...].astype(F32) * w_value, axis=1, keepdims=True)
    vb1[0] = jnp.where(own_line, to_lanes(v_part), 0.0)

    G, S, R = (gs, gr), (ss, sr), (rs, rr)
    both, every = pl.ds(0, 2), pl.ds(0, 8)
    live = {}

    def begin(name, i, *what):
        live[(name, i)] = send(*what)

    def finish(name, n):
        for i in range(1, n + 1):
            live[(name, i)].wait()

    def g_z():
        ref = w2.at[core, both, xl, xh, z, own_rows]
        for i in range(1, 8):
            begin("gz", i, ref, ref, G, i - 1, z_peer(i))

    def g_2():
        finish("gz", 7)
        for i in (1, 2, 3):
            for half, peer, k in ((0, x_peer(i), 6), (1, y_peer(i), 9)):
                ref = w2.at[core, half, xl, xh, every, own_rows]
                begin(f"g2{half}", i, ref, ref, G, k + i, peer)

    def to_core(k, ref):
        begin("gc", k + 1, ref, ref, G, 19 + k, core_id)

    def g_3():
        finish("g20", 3)
        ref = w2.at[core, 0, both, both, every, own_rows]
        for i in (1, 2, 3):
            begin("g30", i, ref, ref, G, 12 + i, y_peer(i))
        to_core(0, ref)
        finish("g21", 3)
        ref = w2.at[core, 1, xl, xh]
        for i in (1, 2, 3):
            begin("g31", i, ref, ref, G, 15 + i, x_peer(i))
        to_core(1, ref)

    def g_end():
        for i in (1, 3, 2):
            live[("g30", i)].wait()
            to_core(1 + i, w2.at[core, 0, both, both, every, rows_of((y + 4 - i) % 4)])
            live[("g31", i)].wait()
            from_h, from_l = x_of(4 - i)
            to_core(4 + i, w2.at[core, 1, from_l, from_h])

    def v_1():
        for i in range(1, 8):
            begin("v1", i, vb1.at[0], vb1.at[i], S, i - 1, xy_peer(i))

    def v_2():
        finish("v1", 7)
        vb2[0] = jnp.sum(vb1[...], axis=0)
        for i in range(1, 8):
            begin("v2", i, vb2.at[0], vb2.at[i], S, 6 + i, z_peer(i))

    def z_1():
        finish("v2", 7)
        v8 = jnp.sum(vb2[...], axis=0)
        rows = []
        for h in range(HEADS):
            w_v = wqkva_v[:, 2 * D + h * HD : 2 * D + (h + 1) * HD].astype(F32)
            col = jnp.sum(w_v * v8[h : h + 1, :], axis=1, keepdims=True)
            rows.append(to_lanes(col))
        zb1[xh, y] = jnp.concatenate(rows, axis=0)
        for i in range(1, 8):
            begin("z1", i, zb1.at[xh, y], zb1.at[xh, y], S, 13 + i, xy_peer(i))

    def z_2():
        finish("z1", 7)
        zb2[z] = jnp.sum(zb1[...], axis=1)
        for i in range(1, 8):
            begin("z2", i, zb2.at[z], zb2.at[z], S, 20 + i, z_peer(i))

    def z_end():
        finish("z2", 7)
        tiles = []
        for i in range(2):
            for j in range(4):
                tiles.append(zb2[2 * j, i] + zb2[2 * j + 1, i])
        z_hi, z_lo = split(jnp.concatenate(tiles, axis=1))
        z128[...] = jnp.zeros((128, D), BF16)
        z128[0:16, :] = jnp.concatenate([z_hi, z_hi], axis=0)
        z128[16:32, :] = jnp.concatenate([z_lo, jnp.zeros_like(z_lo)], axis=0)

    loads[0].wait()
    x = hid[...].astype(F32)
    inv_t = lax.rsqrt(jnp.mean(x * x, axis=1, keepdims=True) + 1e-6)
    norm_t[...] = (x * inv_t * gain_t_v[...]).astype(BF16)
    for j in range(6):
        loads[1 + j].wait()
        at = slice(512 * j, 512 * j + 512)
        qkv[:, at] = nn(norm_t[...], wqkv[:, at]).astype(BF16)
        if j == BAR:
            pl.semaphore_wait(barrier, 18)
            g_z()
            v_1()
    done = done_v[...]
    ri, ci = iota((STEPS, STEPS), 0), iota((STEPS, STEPS), 1)
    allowed_t = (ri >= ci) & ((ri > done) == (ci > done))
    for h in range(HEADS):
        at = slice(h * HD, (h + 1) * HD)
        s = nt(qkv[:, at], qkv[:, D + h * HD : D + (h + 1) * HD]) * SCALE
        s = jnp.where(allowed_t, s, NEG)
        e = jnp.exp(s - jnp.max(s, axis=1, keepdims=True))
        p = (e / jnp.sum(e, axis=1, keepdims=True)).astype(BF16)
        prob_t[h] = p
        mixed[:, at] = nn(p, qkv[:, 2 * D + h * HD : 2 * D + (h + 1) * HD]).astype(BF16)
        if h == V2_AT:
            v_2()
        if h == G2_AT:
            g_2()
    loads[7].wait()
    turn = step_to_block(False)
    for q in range(4):
        at = slice(256 * q, 256 * q + 256)
        h1 = (hid[:, at].astype(F32) + nn(mixed[...], wout[:, at])).astype(BF16)
        for j in range(4):
            stage1[j, q * 64 : q * 64 + 64, :] = h1[j * 64 : j * 64 + 64, :]
    for j in range(4):
        a1[j * 256 : j * 256 + 256, :] = nn(turn, stage1[j]).astype(BF16)

    def block(peer):
        return pl.ds(pl.multiple_of(peer * 16, 16), 16)

    def put_1(peer):
        send(a1.at[block(peer)], r1.at[block(me)], (as1, ar1), 0, {"tm": peer})

    spread(put_1)
    r1[block(me), :] = a1[block(me), :]

    def wait_all(src, dst, sems):
        pltpu.make_async_remote_copy(
            src_ref=src.at[pl.ds(0, 1008)], dst_ref=dst.at[pl.ds(0, 1008)], send_sem=sems[0].at[0],
            recv_sem=sems[1].at[0], device_id=core_id, device_id_type=pl.DeviceIdType.MESH,
        ).wait()

    z_1()
    g_3()
    z_2()
    z_end()
    wait_all(a1, r1, (as1, ar1))

    unturn = block_to_agent(False)
    for j in range(4):
        got = nn(unturn, r1[j * 256 : j * 256 + 256, :]).astype(BF16)
        for q in range(4):
            for s in range(4):
                i = (q * 4 + s) * 16
                xr[s * 64 + j * 16 : s * 64 + j * 16 + 16, q * 256 : q * 256 + 256] = got[
                    i : i + 16, :
                ]
    xa = xr[...].astype(F32)
    inv_a = lax.rsqrt(jnp.mean(xa * xa, axis=1, keepdims=True) + 1e-6)
    h1_value = jnp.sum(xa * w_value, axis=1, keepdims=True)
    normed = xa * inv_a * gain_a_v[...]
    na[...] = normed.astype(BF16)
    for j in range(4):
        nat[0, j * 256 : j * 256 + 256, :] = normed[:, j * 256 : j * 256 + 256].T.astype(BF16)
    begin("nat", 1, nat.at[0], nat.at[1], G, 27, core_id)
    s_rows = nt(z128[0:32, :], na[...])
    s_rows = s_rows[0:8] + s_rows[16:24]
    diag = ri == ci
    alive_row, target_row = rows_v[0:1, :], rows_v[1:2, :]

    def to_column(row):
        return jnp.sum(jnp.where(diag, row, 0.0), axis=1, keepdims=True)

    alive_col, target_col = to_column(alive_row), to_column(target_row)
    g_end()

    def project(which):
        for half in range(2):
            for l in range(2):
                at = half * 512 + l * 256
                w = w2[which, half, l].reshape(D, 256)
                qk[which, :, at : at + 256] = nn(na[...], w).astype(BF16)

    project(core)
    finish("gc", 8)
    project(1 - core)
    square = iota((128, 128), 0), iota((128, 128), 1)
    same_step = (square[0] // 64) == (square[1] // 64)
    sums = []
    for p in range(2):
        rows = slice(128 * p, 128 * p + 128)
        seen = same_step & ((alive_row[:, rows] == 1.0) | (square[0] == square[1]))
        total = jnp.zeros((128, 1), F32)
        for h in range(HEADS):
            at = slice(h * HD, (h + 1) * HD)
            s = nt(qk[0, rows, at], qk[1, rows, at]) * SCALE
            s = jnp.where(seen, s, NEG)
            e = jnp.exp(s - jnp.max(s, axis=1, keepdims=True))
            e = e / jnp.sum(e, axis=1, keepdims=True)
            prob_a[h, p] = e
            total = total + jnp.sum(e * s_rows[h : h + 1, rows], axis=1, keepdims=True)
        sums.append(total)
    predicted = h1_value + jnp.concatenate(sums, axis=0)
    err = 32.0 * alive_col * (predicted - target_col)
    values_o[...] = jnp.sum(jnp.where(diag, predicted, 0.0), axis=0, keepdims=True)
    for p in range(2):
        rows = slice(128 * p, 128 * p + 128)
        for h in range(HEADS):
            at = slice(h * HD, (h + 1) * HD)
            e = prob_a[h, p]
            s_row = s_rows[h : h + 1, rows]
            pv = jnp.sum(e * s_row, axis=1, keepdims=True)
            weighted = e * err[rows, :]
            trow[h : h + 1, rows] = jnp.sum(weighted, axis=0, keepdims=True)
            ds = weighted * (s_row - pv) * SCALE
            dqk[0, rows, at] = nn(ds.astype(BF16), qk[1, rows, at]).astype(BF16)
            dqk[1, rows, at] = nn(ds.T.astype(BF16), qk[0, rows, at]).astype(BF16)
    begin("dqk", 1, dqk.at[1 - core], dqr, G, 28, core_id)

    t_hi = trow[...].astype(BF16).astype(F32)
    t_lo = trow[...] - t_hi
    u_all = nn(jnp.concatenate([t_hi, t_lo], axis=0).astype(BF16), na[...])
    u_all = u_all[0:8] + u_all[8:16]
    for i in range(8):
        for j in range(2):
            at = (j * 4 + i // 2) * 128
            us1[i, j] = u_all[:, at : at + 128]
    for i in range(1, 8):
        begin("uz", i, us1.at[(z + i) % 8], uz.at[i - 1], S, 27 + i, z_peer(i))

    live[("nat", 1)].wait()
    live[("dqk", 1)].wait()
    for half in range(2):
        for l in range(2):
            at = half * 512 + l * 256
            part = nn(nat[0], dqk[core, :, at : at + 256]) + nn(nat[1], dqr[:, at : at + 256])
            tb[half, l] = part.astype(BF16).reshape(2, 8, 64, 256)
        for i in (1, 2, 3):
            if half == 0:
                begin(
                    "p1y", i, tb.at[0, both, both, every, rows_of((y + i) % 4)], p1y.at[i - 1],
                    R, i - 1, y_peer(i),
                )
            else:
                to_h, to_l = x_of(i)
                begin("p1x", i, tb.at[1, to_l, to_h], p1x.at[i - 1], R, 2 + i, x_peer(i))

    t_all = jnp.concatenate([t_hi, t_lo, t_hi, jnp.zeros((104, STEPS), F32)], axis=0)
    t_col = t_all.T.astype(BF16)
    for i in range(4):
        at = slice(256 * i, 256 * i + 256)
        part = nn(t_col, z128[:, at])
        for c in range(2):
            for half in range(2):
                for l in range(2):
                    w = w2[c, half, l, i // 2, 4 * (i % 2) : 4 * (i % 2) + 4].reshape(256, 256)
                    lanes = half * 512 + l * 256
                    part = part + nt(dqk[c, :, lanes : lanes + 256], w)
        gnorm[:, at] = part * gain_a_v[:, at]
    gy = gnorm[...]
    xa = xr[...].astype(F32)
    pull = jnp.mean(xa * gy, axis=1, keepdims=True) * (inv_a * inv_a * inv_a)
    grad = (err * w_value + gy * inv_a - xa * pull).astype(BF16)
    turn = block_to_agent(True)
    for j in range(4):
        for q in range(4):
            for s in range(4):
                i = (q * 4 + s) * 16
                stage2[i : i + 16, j * 256 : j * 256 + 256] = grad[
                    s * 64 + j * 16 : s * 64 + j * 16 + 16, q * 256 : q * 256 + 256
                ]
    for j in range(4):
        a2[j * 256 : j * 256 + 256, :] = nn(turn, stage2[:, j * 256 : j * 256 + 256]).astype(BF16)

    def put_2(peer):
        send(a2.at[block(peer)], r2.at[block(me)], (as2, ar2), 0, {"tm": peer})

    spread(put_2)
    r2[block(me), :] = a2[block(me), :]

    def u_xy():
        finish("uz", 7)
        um[...] = us1[z] + jnp.sum(uz[...], axis=0)
        for i in range(1, 8):
            begin("uxy", i, um.at[xy_of(i)[0]], uxy.at[i - 1], S, 34 + i, xy_peer(i))

    def u_env():
        finish("uxy", 7)
        uf[...] = um[xh] + jnp.sum(uxy[...], axis=0)
        for i in (1, 2, 3):
            begin("ue", i, uf, ue.at[i - 1], S, 41 + i, {"env": (env + i) % 4})

    def u_mix():
        finish("ue", 3)
        u = uf[...] + jnp.sum(ue[...], axis=0)
        v8 = jnp.sum(vb2[...], axis=0)
        lines = []
        for h in range(HEADS):
            at = slice(2 * D + h * HD, 2 * D + (h + 1) * HD)
            col = jnp.sum(jnp.where(spot, u[h : h + 1, :], 0.0), axis=1, keepdims=True)
            qkvg_o[:, at] = col * v8[h : h + 1, :]
            lines.append(jnp.sum(col * wqkva_v[:, at].astype(F32), axis=0, keepdims=True))
        up[...] = jnp.concatenate(lines, axis=0)
        for i in range(1, 8):
            begin("uq", i, up, uq.at[i - 1], S, 44 + i, z_peer(i))

    def u_last():
        finish("uq", 7)
        uw[...] = up[...] + jnp.sum(uq[...], axis=0)
        for i in range(1, 8):
            begin("ux", i, uw, ux.at[i - 1], S, 51 + i, xy_peer(i))

    def u_end():
        finish("ux", 7)
        total = uw[...] + jnp.sum(ux[...], axis=0)
        row = jnp.sum(jnp.where(own_line, total, 0.0), axis=0, keepdims=True)
        outg_o[...] = jnp.sum(jnp.where(spot, row, 0.0), axis=1, keepdims=True) * w_value

    def r_2():
        finish("p1y", 3)
        for l in range(2):
            for i in range(2):
                total = tb[0, l, i, :, own_rows, :].astype(F32)
                for k in range(3):
                    total = total + p1y[k, l, i].astype(F32)
                s1[l, i] = total.astype(BF16)
        for i in (1, 2, 3):
            to_h, to_l = x_of(i)
            begin("p2x", i, s1.at[to_l, to_h], p2x.at[i - 1], R, 5 + i, x_peer(i))
        finish("p1x", 3)
        for i in range(8):
            total = tb[1, xl, xh, i].astype(F32)
            for k in range(3):
                total = total + p1x[k, i].astype(F32)
            s2[i] = total.astype(BF16)
        for i in (1, 2, 3):
            begin(
                "p2y", i, s2.at[every, rows_of((y + i) % 4)], p2y.at[i - 1], R, 8 + i, y_peer(i)
            )

    def r_z():
        finish("p2x", 3)
        total = s1[xl, xh].astype(F32)
        for k in range(3):
            total = total + p2x[k].astype(F32)
        s3[0] = total.astype(BF16)
        finish("p2y", 3)
        total = s2[:, own_rows, :].astype(F32)
        for k in range(3):
            total = total + p2y[k].astype(F32)
        s3[1] = total.astype(BF16)
        for i in range(1, 8):
            begin("pz", i, s3.at[both, (z + i) % 8], pz.at[i - 1], R, 11 + i, z_peer(i))

    def r_env():
        finish("pz", 7)
        total = s3[:, z].astype(F32)
        for k in range(7):
            total = total + pz[k].astype(F32)
        eb[env] = total
        for i in (1, 2, 3):
            begin("eb", i, eb.at[env], eb.at[env], R, 18 + i, {"env": (env + i) % 4})

    def r_end():
        finish("eb", 3)
        for e in range(4):
            for half in range(2):
                at = (e % 2) * D + half * 512 + (e // 2) * 256
                qkvg_o[:, at : at + 256] = eb[e, half]

    u_xy()
    u_env()

    wait_all(a2, r2, (as2, ar2))
    unturn = step_to_block(True)
    for j in range(4):
        got = nn(unturn, r2[j * 256 : j * 256 + 256, :]).astype(BF16)
        for q in range(4):
            gh[j * 64 : j * 64 + 64, q * 256 : q * 256 + 256] = got[q * 64 : q * 64 + 64, :]
    u_mix()
    after = {0: r_2, 3: u_last, 7: r_z}
    for h in range(HEADS):
        at = slice(h * HD, (h + 1) * HD)
        at_k, at_v = slice(D + h * HD, D + (h + 1) * HD), slice(2 * D + h * HD, 2 * D + (h + 1) * HD)
        gm = nt(gh[...], wout[at, :]).astype(BF16)
        p = prob_t[h]
        pf = p.astype(F32)
        dp = nt(gm, qkv[:, at_v])
        ds = (pf * (dp - jnp.sum(pf * dp, axis=1, keepdims=True)) * SCALE)
        q_h, k_h = qkv[:, at], qkv[:, at_k]
        qkv[:, at_v] = nn(pf.T.astype(BF16), gm).astype(BF16)
        qkv[:, at] = nn(ds.astype(BF16), k_h).astype(BF16)
        qkv[:, at_k] = nn(ds.T.astype(BF16), q_h).astype(BF16)
        if h in after:
            after[h]()
    for i in range(4):
        at = slice(256 * i, 256 * i + 256)
        gnorm[:, at] = nt(qkv[...], wqkv[at, :]) * gain_t_v[:, at]
    gy = gnorm[...]
    x = hid[...].astype(F32)
    inv_t = lax.rsqrt(jnp.mean(x * x, axis=1, keepdims=True) + 1e-6)
    pull = jnp.mean(x * gy, axis=1, keepdims=True) * (inv_t * inv_t * inv_t)
    igrad_o[...] = (gh[...].astype(F32) + gy * inv_t - x * pull).astype(BF16)
    u_end()
    r_env()
    r_end()


def per_device(
    hidden, done_step, alive, targets, gain_t, w_qkv_t, w_out_t, gain_a, w_qkv_a, w_out_a, w_value
):
    rows = jnp.stack([alive[0].astype(F32).T.reshape(-1), targets[0].T.reshape(-1)])
    vmem = pl.BlockSpec(memory_space=pltpu.VMEM)
    away = pl.BlockSpec(memory_space=pl.ANY)
    mem = pltpu.VMEM
    dma = pltpu.SemaphoreType.DMA
    tile = (8, 128)
    scratch = [
        mem((STEPS, D), BF16), mem((D, 3 * D), BF16), mem((D, D), BF16), mem((STEPS, D), BF16),
        mem((STEPS, 3 * D), BF16), mem((HEADS, STEPS, STEPS), BF16), mem((STEPS, D), BF16),
        mem((4, 256, 256), BF16), mem((1024, 256), BF16), mem((1024, 256), BF16),
        mem((STEPS, D), BF16),
        mem((2, 2, 2, 2, 8, 64, 256), BF16), mem((8, *tile), F32), mem((8, *tile), F32),
        mem((2, 4, *tile), F32), mem((8, 2, *tile), F32), mem((128, D), BF16),
        mem((STEPS, D), BF16), mem((2, D, STEPS), BF16), mem((2, STEPS, D), BF16),
        mem((HEADS, 2, 128, 128), F32), mem((2, STEPS, D), BF16), mem((STEPS, D), BF16),
        mem((HEADS, STEPS), F32), mem((STEPS, D), F32), mem((256, 1024), BF16),
        mem((1024, 256), BF16), mem((1024, 256), BF16), mem((STEPS, D), BF16),
        mem((2, 2, 2, 8, 64, 256), BF16), mem((3, 2, 2, 8, 16, 256), BF16),
        mem((3, 8, 64, 256), BF16), mem((2, 2, 8, 16, 256), BF16), mem((8, 64, 256), BF16),
        mem((3, 8, 16, 256), BF16), mem((3, 8, 16, 256), BF16), mem((2, 8, 16, 256), BF16),
        mem((7, 2, 16, 256), BF16), mem((4, 2, 16, 256), F32),
        mem((8, 2, *tile), F32), mem((7, 2, *tile), F32), mem((2, *tile), F32),
        mem((7, *tile), F32), mem(tile, F32), mem((3, *tile), F32), mem(tile, F32),
        mem((7, *tile), F32), mem(tile, F32), mem((7, *tile), F32),
        dma((8,)), dma((29,)), dma((29,)), dma((1,)), dma((1,)), dma((1,)), dma((1,)),
        dma((59,)), dma((59,)), dma((22,)), dma((22,)),
    ]
    values, input_grad, qkv_grad, out_grad = pl.pallas_call(
        kernel,
        out_shape=(
            jax.ShapeDtypeStruct((1, STEPS), F32),
            jax.ShapeDtypeStruct((STEPS, D), BF16),
            jax.ShapeDtypeStruct((16, 3 * D), F32),
            jax.ShapeDtypeStruct((16, D), F32),
        ),
        in_specs=[away, vmem, vmem, vmem, away, away, vmem, vmem, vmem, vmem],
        out_specs=(vmem, vmem, vmem, vmem),
        scratch_shapes=scratch,
        compiler_params=pltpu.CompilerParams(
            collective_id=0, has_side_effects=True, vmem_limit_bytes=60 * 2**20
        ),
    )(
        hidden[0, 0], done_step, rows, gain_t[None], w_qkv_t, w_out_t, gain_a[None], w_qkv_a,
        w_out_a, w_value[None],
    )
    values = values.reshape(-1, AGENTS).T
    return values[None], input_grad[None, None], qkv_grad, out_grad


def solution(mesh):
    in_specs = (
        P("env", "tm", None, None),
        P("env", "tm"),
        P("env", None, "tm"),
        P("env", None, "tm"),
        P(),
        P(),
        P(),
        P(),
        P("tm", None),
        P("tm", None),
        P(),
    )
    out_specs = (P("env", None, "tm"), P("env", "tm", None, None), P("tm", None), P("tm", None))
    return jax.shard_map(
        per_device, mesh=mesh, in_specs=in_specs, out_specs=out_specs, check_vma=False
    )
```

time: 132 us -> 103 us (0.78)
  the two profiles are of different devices: /device:TPU:8 before, /device:TPU:1 now
where the time goes in v3:
time: 103 us
  Pallas kernels  92.1 us (89%)
  local copies, waits for them, and re-layouts  6.98 us (7%)
  other arithmetic  2.6 us (3%)
  between operations  1.29 us (1%)
    pallas_call x1, Pallas kernels, per_device(): pl.pallas_call(kernel, out_shape=(jax.ShapeDtypeStruct((1, STEPS), F32),...  92.1 us
    unnamed x3, local copies, waits for them, and re-layouts  4.96 us

profile of v3, /device:TPU:1, one launch (start us, length us, event | category | flops | bytes accessed | tf_op | source)
XLA Modules:
  0.0 103.0 jit_solution(2825284714622335735)
XLA Ops:
  1.3 0.8 stack_reshape.7
  2.0 0.7 convert_bitcast_fusion
  2.7 0.1 stack_reshape.6
  2.8 0.6 pad_maximum_fusion.rows_v
  3.4 92.1 %shard_map.138 = (f32[1,256]{1,0:T(1,128)}, bf16[256,1024]{1,0:T(8,128)(2,1)}, f32[16,3072]{1,0:T(8,128)}, f32[16,1024]{1,0:T(8,128)}) custom-call(bf16[256,1024]{1,0:T(8,128)(2,1)} %bitcast.15, s32[1,1]{1,0:T(1,128)S(6)} %copy.18.done_v, f32[2,256]{1,0:T(2,128)} %pad_maximum_fusion.rows_v, f32[1,1024]{1,0:T(1,128)} %bitcast.17, bf16[1024,3072]{1,0:T(8,128)(2,1)} %wqkv_h.1, ...), custom_call_target="tpu_custom_call" | custom-call | tf_op jit(solution)/shard_map/pallas_call | solution.py:584
  95.5 0.5 broadcast.3
  96.0 1.3 %reduce.3 = f32[256]{0:T(256)S(1)} reduce(f32[1,256]{1,0:T(1,128)} %get-tuple-element.8, f32[]{:T(128)} %broadcast.3), dimensions={0}, to_apply=%get-tuple-element.8.reduce_sub_computation.3 | reduce | bytes 2052 | tf_op jit(solution)/shard_map/pallas_call | solution.py:584
  97.4 0.7 reshape.12
  98.0 1.9 %copy.19 = bf16[1,1,256,1024]{3,2,1,0:T(8,128)(2,1)} copy(bf16[1,1,256,1024]{3,2,1,0:T(8,128)(2,1)} %bitcast.16) | data formatting | bytes 1048576
  99.9 1.6 %copy.20 = f32[16,3072]{1,0:T(8,128)} copy(f32[16,3072]{1,0:T(8,128)} %get-tuple-element.18) | data formatting | bytes 393216
  101.5 1.5 %copy.21 = f32[16,1024]{1,0:T(8,128)} copy(f32[16,1024]{1,0:T(8,128)} %get-tuple-element.19) | data formatting | bytes 131072

commit v4 on v3

--- a/solution.py
+++ b/solution.py
@@ -55,11 +55,11 @@
 
 
 def kernel(
-    hidden_h, done_v, rows_v, gain_t_v, wqkv_h, wout_h, gain_a_v, wqkva_v, wouta_v, wval_v,
+    hidden_h, done_v, alive_v, target_v, gain_t_v, wqkv_h, wout_h, gain_a_v, wqkva_v, wouta_v, wval_v,
     values_o, igrad_o, qkvg_o, outg_o,
     hid, wqkv, wout, norm_t, qkv, prob_t, mixed, stage1, a1, r1, xr,
     w2, vb1, vb2, zb1, zb2, z128, na, nat, qk, prob_a, dqk, dqr, trow, gnorm, stage2, a2, r2, gh,
-    tb, p1y, p1x, s1, s2, p2x, p2y, s3, pz, eb, us1, uz, um, uxy, uf, ue, up, uq, uw, ux,
+    tb, opp_y, opp_x, p1y, p1x, s1, s2, p2x, p2y, s3, pz, eb, us1, uz, um, uxy, uf, ue, up, uq, uw, ux,
     lsem, gs, gr, as1, ar1, as2, ar2, ss, sr, rs, rr,
 ):
     me, env = lax.axis_index("tm"), lax.axis_index("env")
@@ -172,27 +172,39 @@
                 begin(f"g2{half}", i, ref, ref, G, k + i, peer)
 
     def to_core(k, ref):
-        begin("gc", k + 1, ref, ref, G, 19 + k, core_id)
+        begin("gc", k + 1, ref, ref, G, 21 + k, core_id)
+
+    first, second = pl.ds(0, 4), pl.ds(4, 4)
+
+    def y_piece(i, zs_=every):
+        return w2.at[core, 0, both, both, zs_, rows_of((y + i) % 4)]
+
+    def x_piece(i, zs_=every):
+        to_h, to_l = x_of(i)
+        return w2.at[core, 1, to_l, to_h, zs_]
 
     def g_3():
-        finish("g20", 3)
-        ref = w2.at[core, 0, both, both, every, own_rows]
-        for i in (1, 2, 3):
-            begin("g30", i, ref, ref, G, 12 + i, y_peer(i))
-        to_core(0, ref)
-        finish("g21", 3)
-        ref = w2.at[core, 1, xl, xh]
-        for i in (1, 2, 3):
-            begin("g31", i, ref, ref, G, 15 + i, x_peer(i))
-        to_core(1, ref)
+        for half, part, peer in ((0, y_piece, y_peer), (1, x_piece, x_peer)):
+            finish(f"g2{half}", 3)
+            for i in (1, 3):
+                begin(f"g3{half}", i, part(0), part(0), G, 13 + 4 * half + i // 2, peer(i))
+            to_core(4 * half, part(0))
+
+    def g_mid():
+        for half, part, peer in ((0, y_piece, y_peer), (1, x_piece, x_peer)):
+            for i, zs_ in ((1, first), (3, second)):
+                live[(f"g3{half}", i)].wait()
+                ref = part(4 - i, zs_)
+                begin(f"g4{half}", i, ref, ref, G, 15 + 4 * half + i // 2, peer(i))
+        for half, part in ((0, y_piece), (1, x_piece)):
+            for i in (1, 3):
+                to_core(4 * half + 1 + i // 2, part(4 - i))
 
     def g_end():
-        for i in (1, 3, 2):
-            live[("g30", i)].wait()
-            to_core(1 + i, w2.at[core, 0, both, both, every, rows_of((y + 4 - i) % 4)])
-            live[("g31", i)].wait()
-            from_h, from_l = x_of(4 - i)
-            to_core(4 + i, w2.at[core, 1, from_l, from_h])
+        for half, part in ((0, y_piece), (1, x_piece)):
+            for i in (1, 3):
+                live[(f"g4{half}", i)].wait()
+            to_core(4 * half + 3, part(2))
 
     def v_1():
         for i in range(1, 8):
@@ -288,6 +300,7 @@
     z_1()
     g_3()
     z_2()
+    g_mid()
     z_end()
     wait_all(a1, r1, (as1, ar1))
 
@@ -307,16 +320,20 @@
     na[...] = normed.astype(BF16)
     for j in range(4):
         nat[0, j * 256 : j * 256 + 256, :] = normed[:, j * 256 : j * 256 + 256].T.astype(BF16)
-    begin("nat", 1, nat.at[0], nat.at[1], G, 27, core_id)
+    begin("nat", 1, nat.at[0], nat.at[1], G, 29, core_id)
     s_rows = nt(z128[0:32, :], na[...])
     s_rows = s_rows[0:8] + s_rows[16:24]
     diag = ri == ci
-    alive_row, target_row = rows_v[0:1, :], rows_v[1:2, :]
+    alive_f, target_f = alive_v[...].astype(F32), target_v[...]
+
+    def one_row(table):
+        return jnp.concatenate([table[s : s + 1, :] for s in range(4)], axis=1)
 
     def to_column(row):
         return jnp.sum(jnp.where(diag, row, 0.0), axis=1, keepdims=True)
 
-    alive_col, target_col = to_column(alive_row), to_column(target_row)
+    alive_row = one_row(alive_f)
+    alive_col, target_col = to_column(alive_row), to_column(one_row(target_f))
     g_end()
 
     def project(which):
@@ -347,7 +364,9 @@
         sums.append(total)
     predicted = h1_value + jnp.concatenate(sums, axis=0)
     err = 32.0 * alive_col * (predicted - target_col)
-    values_o[...] = jnp.sum(jnp.where(diag, predicted, 0.0), axis=0, keepdims=True)
+    line = jnp.sum(jnp.where(diag, predicted, 0.0), axis=0, keepdims=True)
+    for s in range(4):
+        values_o[s : s + 1, :] = line[:, s * 64 : s * 64 + 64]
     for p in range(2):
         rows = slice(128 * p, 128 * p + 128)
         for h in range(HEADS):
@@ -360,7 +379,7 @@
             ds = weighted * (s_row - pv) * SCALE
             dqk[0, rows, at] = nn(ds.astype(BF16), qk[1, rows, at]).astype(BF16)
             dqk[1, rows, at] = nn(ds.T.astype(BF16), qk[0, rows, at]).astype(BF16)
-    begin("dqk", 1, dqk.at[1 - core], dqr, G, 28, core_id)
+    begin("dqk", 1, dqk.at[1 - core], dqr, G, 30, core_id)
 
     t_hi = trow[...].astype(BF16).astype(F32)
     t_lo = trow[...] - t_hi
@@ -372,23 +391,6 @@
             us1[i, j] = u_all[:, at : at + 128]
     for i in range(1, 8):
         begin("uz", i, us1.at[(z + i) % 8], uz.at[i - 1], S, 27 + i, z_peer(i))
-
-    live[("nat", 1)].wait()
-    live[("dqk", 1)].wait()
-    for half in range(2):
-        for l in range(2):
-            at = half * 512 + l * 256
-            part = nn(nat[0], dqk[core, :, at : at + 256]) + nn(nat[1], dqr[:, at : at + 256])
-            tb[half, l] = part.astype(BF16).reshape(2, 8, 64, 256)
-        for i in (1, 2, 3):
-            if half == 0:
-                begin(
-                    "p1y", i, tb.at[0, both, both, every, rows_of((y + i) % 4)], p1y.at[i - 1],
-                    R, i - 1, y_peer(i),
-                )
-            else:
-                to_h, to_l = x_of(i)
-                begin("p1x", i, tb.at[1, to_l, to_h], p1x.at[i - 1], R, 2 + i, x_peer(i))
 
     t_all = jnp.concatenate([t_hi, t_lo, t_hi, jnp.zeros((104, STEPS), F32)], axis=0)
     t_col = t_all.T.astype(BF16)
@@ -402,6 +404,34 @@
                     lanes = half * 512 + l * 256
                     part = part + nt(dqk[c, :, lanes : lanes + 256], w)
         gnorm[:, at] = part * gain_a_v[:, at]
+
+    peers, opp = (y_peer, x_peer), (opp_y, opp_x)
+
+    def term(half, i, zs_):
+        if half == 0:
+            return tb.at[0, both, both, zs_, rows_of((y + i) % 4)]
+        to_h, to_l = x_of(i)
+        return tb.at[1, to_l, to_h, zs_]
+
+    def got_1(half, n, zs_):
+        return p1y.at[n, both, both, zs_] if half == 0 else p1x.at[n, zs_]
+
+    live[("nat", 1)].wait()
+    live[("dqk", 1)].wait()
+    for half in range(2):
+        for l in range(2):
+            at = half * 512 + l * 256
+            part = nn(nat[0], dqk[core, :, at : at + 256]) + nn(nat[1], dqr[:, at : at + 256])
+            tb[half, l] = part.astype(BF16).reshape(2, 8, 64, 256)
+        for n, (i, across, plain) in enumerate(((1, first, second), (3, second, first))):
+            begin(
+                f"q{half}", i, term(half, 2, across), opp[half].at[n], R, 6 * half + n, peers[half](i)
+            )
+            begin(
+                f"p{half}", i, term(half, i, plain), got_1(half, n, plain),
+                R, 6 * half + 2 + n, peers[half](i),
+            )
+
     gy = gnorm[...]
     xa = xr[...].astype(F32)
     pull = jnp.mean(xa * gy, axis=1, keepdims=True) * (inv_a * inv_a * inv_a)
@@ -461,26 +491,50 @@
         row = jnp.sum(jnp.where(own_line, total, 0.0), axis=0, keepdims=True)
         outg_o[...] = jnp.sum(jnp.where(spot, row, 0.0), axis=1, keepdims=True) * w_value
 
+    def r_1():
+        for half in range(2):
+            for n, (i, across) in enumerate(((1, first), (3, second))):
+                live[(f"q{half}", i)].wait()
+                z0 = 4 * n
+                if half == 0:
+                    rows = rows_of((y + i) % 4)
+                    for l in range(2):
+                        for k in range(2):
+                            both_terms = tb[0, l, k, z0 : z0 + 4, rows, :] + opp_y[n, l, k]
+                            tb[0, l, k, z0 : z0 + 4, rows, :] = both_terms
+                else:
+                    to_h, to_l = x_of(i)
+                    for k in range(4):
+                        tb[1, to_l, to_h, z0 + k] = tb[1, to_l, to_h, z0 + k] + opp_x[n, k]
+                begin(
+                    f"r{half}", i, term(half, i, across), got_1(half, n, across),
+                    R, 6 * half + 4 + n, peers[half](i),
+                )
+
     def r_2():
-        finish("p1y", 3)
+        for name in ("p0", "r0"):
+            for i in (1, 3):
+                live[(name, i)].wait()
         for l in range(2):
             for i in range(2):
                 total = tb[0, l, i, :, own_rows, :].astype(F32)
-                for k in range(3):
+                for k in range(2):
                     total = total + p1y[k, l, i].astype(F32)
                 s1[l, i] = total.astype(BF16)
         for i in (1, 2, 3):
             to_h, to_l = x_of(i)
-            begin("p2x", i, s1.at[to_l, to_h], p2x.at[i - 1], R, 5 + i, x_peer(i))
-        finish("p1x", 3)
+            begin("p2x", i, s1.at[to_l, to_h], p2x.at[i - 1], R, 11 + i, x_peer(i))
+        for name in ("p1", "r1"):
+            for i in (1, 3):
+                live[(name, i)].wait()
         for i in range(8):
             total = tb[1, xl, xh, i].astype(F32)
-            for k in range(3):
+            for k in range(2):
                 total = total + p1x[k, i].astype(F32)
             s2[i] = total.astype(BF16)
         for i in (1, 2, 3):
             begin(
-                "p2y", i, s2.at[every, rows_of((y + i) % 4)], p2y.at[i - 1], R, 8 + i, y_peer(i)
+                "p2y", i, s2.at[every, rows_of((y + i) % 4)], p2y.at[i - 1], R, 14 + i, y_peer(i)
             )
 
     def r_z():
@@ -495,7 +549,7 @@
             total = total + p2y[k].astype(F32)
         s3[1] = total.astype(BF16)
         for i in range(1, 8):
-            begin("pz", i, s3.at[both, (z + i) % 8], pz.at[i - 1], R, 11 + i, z_peer(i))
+            begin("pz", i, s3.at[both, (z + i) % 8], pz.at[i - 1], R, 17 + i, z_peer(i))
 
     def r_env():
         finish("pz", 7)
@@ -504,7 +558,7 @@
             total = total + pz[k].astype(F32)
         eb[env] = total
         for i in (1, 2, 3):
-            begin("eb", i, eb.at[env], eb.at[env], R, 18 + i, {"env": (env + i) % 4})
+            begin("eb", i, eb.at[env], eb.at[env], R, 24 + i, {"env": (env + i) % 4})
 
     def r_end():
         finish("eb", 3)
@@ -513,7 +567,9 @@
                 at = (e % 2) * D + half * 512 + (e // 2) * 256
                 qkvg_o[:, at : at + 256] = eb[e, half]
 
+    r_1()
     u_xy()
+    r_2()
     u_env()
 
     wait_all(a2, r2, (as2, ar2))
@@ -522,8 +578,7 @@
         got = nn(unturn, r2[j * 256 : j * 256 + 256, :]).astype(BF16)
         for q in range(4):
             gh[j * 64 : j * 64 + 64, q * 256 : q * 256 + 256] = got[q * 64 : q * 64 + 64, :]
-    u_mix()
-    after = {0: r_2, 3: u_last, 7: r_z}
+    after = {1: r_z, 2: u_mix, 5: u_last}
     for h in range(HEADS):
         at = slice(h * HD, (h + 1) * HD)
         at_k, at_v = slice(D + h * HD, D + (h + 1) * HD), slice(2 * D + h * HD, 2 * D + (h + 1) * HD)
@@ -538,6 +593,7 @@
         qkv[:, at_k] = nn(ds.T.astype(BF16), q_h).astype(BF16)
         if h in after:
             after[h]()
+    r_env()
     for i in range(4):
         at = slice(256 * i, 256 * i + 256)
         gnorm[:, at] = nt(qkv[...], wqkv[at, :]) * gain_t_v[:, at]
@@ -547,14 +603,17 @@
     pull = jnp.mean(x * gy, axis=1, keepdims=True) * (inv_t * inv_t * inv_t)
     igrad_o[...] = (gh[...].astype(F32) + gy * inv_t - x * pull).astype(BF16)
     u_end()
-    r_env()
     r_end()
+
+
+def hand_on(*refs):
+    for i in range(4):
+        refs[4 + i][...] = refs[i][...]
 
 
 def per_device(
     hidden, done_step, alive, targets, gain_t, w_qkv_t, w_out_t, gain_a, w_qkv_a, w_out_a, w_value
 ):
-    rows = jnp.stack([alive[0].astype(F32).T.reshape(-1), targets[0].T.reshape(-1)])
     vmem = pl.BlockSpec(memory_space=pltpu.VMEM)
     away = pl.BlockSpec(memory_space=pl.ANY)
     mem = pltpu.VMEM
@@ -571,36 +630,39 @@
         mem((HEADS, 2, 128, 128), F32), mem((2, STEPS, D), BF16), mem((STEPS, D), BF16),
         mem((HEADS, STEPS), F32), mem((STEPS, D), F32), mem((256, 1024), BF16),
         mem((1024, 256), BF16), mem((1024, 256), BF16), mem((STEPS, D), BF16),
-        mem((2, 2, 2, 8, 64, 256), BF16), mem((3, 2, 2, 8, 16, 256), BF16),
-        mem((3, 8, 64, 256), BF16), mem((2, 2, 8, 16, 256), BF16), mem((8, 64, 256), BF16),
+        mem((2, 2, 2, 8, 64, 256), BF16), mem((2, 2, 2, 4, 16, 256), BF16),
+        mem((2, 4, 64, 256), BF16), mem((2, 2, 2, 8, 16, 256), BF16), mem((2, 8, 64, 256), BF16), mem((2, 2, 8, 16, 256), BF16), mem((8, 64, 256), BF16),
         mem((3, 8, 16, 256), BF16), mem((3, 8, 16, 256), BF16), mem((2, 8, 16, 256), BF16),
         mem((7, 2, 16, 256), BF16), mem((4, 2, 16, 256), F32),
         mem((8, 2, *tile), F32), mem((7, 2, *tile), F32), mem((2, *tile), F32),
         mem((7, *tile), F32), mem(tile, F32), mem((3, *tile), F32), mem(tile, F32),
         mem((7, *tile), F32), mem(tile, F32), mem((7, *tile), F32),
-        dma((8,)), dma((29,)), dma((29,)), dma((1,)), dma((1,)), dma((1,)), dma((1,)),
-        dma((59,)), dma((59,)), dma((22,)), dma((22,)),
+        dma((8,)), dma((31,)), dma((31,)), dma((1,)), dma((1,)), dma((1,)), dma((1,)),
+        dma((59,)), dma((59,)), dma((28,)), dma((28,)),
     ]
-    values, input_grad, qkv_grad, out_grad = pl.pallas_call(
-        kernel,
-        out_shape=(
-            jax.ShapeDtypeStruct((1, STEPS), F32),
+    shapes = (
+            jax.ShapeDtypeStruct((4, AGENTS), F32),
             jax.ShapeDtypeStruct((STEPS, D), BF16),
             jax.ShapeDtypeStruct((16, 3 * D), F32),
             jax.ShapeDtypeStruct((16, D), F32),
-        ),
-        in_specs=[away, vmem, vmem, vmem, away, away, vmem, vmem, vmem, vmem],
+    )
+    results = pl.pallas_call(
+        kernel,
+        out_shape=shapes,
+        in_specs=[away, vmem, vmem, vmem, vmem, away, away, vmem, vmem, vmem, vmem],
         out_specs=(vmem, vmem, vmem, vmem),
         scratch_shapes=scratch,
         compiler_params=pltpu.CompilerParams(
             collective_id=0, has_side_effects=True, vmem_limit_bytes=60 * 2**20
         ),
     )(
-        hidden[0, 0], done_step, rows, gain_t[None], w_qkv_t, w_out_t, gain_a[None], w_qkv_a,
+        hidden[0, 0], done_step, alive[0].T, targets[0].T, gain_t[None], w_qkv_t, w_out_t, gain_a[None], w_qkv_a,
         w_out_a, w_value[None],
     )
-    values = values.reshape(-1, AGENTS).T
-    return values[None], input_grad[None, None], qkv_grad, out_grad
+    values, input_grad, qkv_grad, out_grad = pl.pallas_call(
+        hand_on, out_shape=shapes, in_specs=[vmem] * 4, out_specs=(vmem,) * 4
+    )(*results)
+    return values.T[None], input_grad[None, None], qkv_grad, out_grad
 
 
 def solution(mesh):

time: 103 us -> 85.1 us (0.83)
  Pallas kernels: 92.1 us -> 83.7 us
  local copies, waits for them, and re-layouts: 6.98 us -> 0 us
  other arithmetic: 2.6 us -> 0 us
    pallas_call x1 -> x2, Pallas kernels: 92.1 us -> 83.7 us  [the longest x1 81.7 us: per_device(): pl.pallas_call(kernel, out_shape=shapes, in_specs=[away, vmem, vmem, vmem...]
    unnamed x3 -> x0, local copies, waits for them, and re-layouts: 4.96 us -> none
    pallas_call x1 -> x0, other arithmetic: 1.33 us -> none  [per_device(): pl.pallas_call(kernel, out_shape=(jax.ShapeDtypeStruct((1, STEPS), F32),...]
where the time goes in v4:
time: 85.1 us; the launch traced here: 85 us
  Pallas kernels  83.7 us (98%)
  between operations  1.29 us (2%)
    pallas_call x1, Pallas kernels, per_device(): pl.pallas_call(kernel, out_shape=shapes, in_specs=[away, vmem, vmem, vmem...  81.7 us
    pallas_call x1, Pallas kernels, per_device(): pl.pallas_call(hand_on, out_shape=shapes, in_specs=[vmem] * 4, out_specs=...  2 us

profile of v4, /device:TPU:1, one launch (start us, length us, event | category | flops | bytes accessed | tf_op | source)
XLA Modules:
  0.0 85.0 jit_solution(10193966857269124058)
XLA Ops:
  1.3 81.7 %shard_map.138 = (f32[4,64]{1,0:T(4,128)}, bf16[256,1024]{1,0:T(8,128)(2,1)}, f32[16,3072]{1,0:T(8,128)}, f32[16,1024]{1,0:T(8,128)}) custom-call(bf16[256,1024]{1,0:T(8,128)(2,1)} %bitcast.14, s32[1,1]{1,0:T(1,128)S(6)} %copy.15.done_v, s32[4,64]{1,0:T(4,128)} %bitcast.18, f32[4,64]{1,0:T(4,128)} %bitcast.19, f32[1,1024]{1,0:T(1,128)} %bitcast.15, ...), custom_call_target="tpu_custom_call" | custom-call | tf_op jit(solution)/shard_map/pallas_call | solution.py:649
  83.0 2.0 %shard_map.139 = (f32[4,64]{1,0:T(4,128)}, bf16[256,1024]{1,0:T(8,128)(2,1)}, f32[16,3072]{1,0:T(8,128)}, f32[16,1024]{1,0:T(8,128)}) custom-call(f32[4,64]{1,0:T(4,128)} %get-tuple-element.12.refs_0_, bf16[256,1024]{1,0:T(8,128)(2,1)} %get-tuple-element.13.refs_1_, f32[16,3072]{1,0:T(8,128)} %get-tuple-element.14.refs_2_, f32[16,1024]{1,0:T(8,128)} %get-tuple-element.15.refs_3_), custom_call_target="tpu_custom_call" | custom-call | tf_op jit(solution)/shard_map/pallas_call | solution.py:662

commit v5 on v4

--- a/solution.py
+++ b/solution.py
@@ -12,7 +12,7 @@
 HD = D // HEADS
 SCALE = 1.0 / math.sqrt(HD)
 NEG = -1e30
-BAR, V2_AT, G2_AT = 5, 3, 7
+BAR, V2_AT, G2_AT = 4, 2, 7
 
 
 def dot(a, b, ca, cb):
@@ -265,7 +265,7 @@
         s = nt(qkv[:, at], qkv[:, D + h * HD : D + (h + 1) * HD]) * SCALE
         s = jnp.where(allowed_t, s, NEG)
         e = jnp.exp(s - jnp.max(s, axis=1, keepdims=True))
-        p = (e / jnp.sum(e, axis=1, keepdims=True)).astype(BF16)
+        p = (e * (1.0 / jnp.sum(e, axis=1, keepdims=True))).astype(BF16)
         prob_t[h] = p
         mixed[:, at] = nn(p, qkv[:, 2 * D + h * HD : 2 * D + (h + 1) * HD]).astype(BF16)
         if h == V2_AT:
@@ -297,8 +297,8 @@
             recv_sem=sems[1].at[0], device_id=core_id, device_id_type=pl.DeviceIdType.MESH,
         ).wait()
 
+    g_3()
     z_1()
-    g_3()
     z_2()
     g_mid()
     z_end()
@@ -358,7 +358,7 @@
             s = nt(qk[0, rows, at], qk[1, rows, at]) * SCALE
             s = jnp.where(seen, s, NEG)
             e = jnp.exp(s - jnp.max(s, axis=1, keepdims=True))
-            e = e / jnp.sum(e, axis=1, keepdims=True)
+            e = e * (1.0 / jnp.sum(e, axis=1, keepdims=True))
             prob_a[h, p] = e
             total = total + jnp.sum(e * s_rows[h : h + 1, rows], axis=1, keepdims=True)
         sums.append(total)
@@ -368,18 +368,18 @@
     for s in range(4):
         values_o[s : s + 1, :] = line[:, s * 64 : s * 64 + 64]
     for p in range(2):
-        rows = slice(128 * p, 128 * p + 128)
+        rows = pl.ds(128 * p, 128)
         for h in range(HEADS):
             at = slice(h * HD, (h + 1) * HD)
             e = prob_a[h, p]
-            s_row = s_rows[h : h + 1, rows]
+            s_row = s_rows[h : h + 1, 128 * p : 128 * p + 128]
             pv = jnp.sum(e * s_row, axis=1, keepdims=True)
-            weighted = e * err[rows, :]
+            weighted = e * err[128 * p : 128 * p + 128, :]
             trow[h : h + 1, rows] = jnp.sum(weighted, axis=0, keepdims=True)
             ds = weighted * (s_row - pv) * SCALE
             dqk[0, rows, at] = nn(ds.astype(BF16), qk[1, rows, at]).astype(BF16)
             dqk[1, rows, at] = nn(ds.T.astype(BF16), qk[0, rows, at]).astype(BF16)
-    begin("dqk", 1, dqk.at[1 - core], dqr, G, 30, core_id)
+        begin("dqk", p + 1, dqk.at[1 - core, rows], dqr.at[rows], G, 30 + p, core_id)
 
     t_hi = trow[...].astype(BF16).astype(F32)
     t_lo = trow[...] - t_hi
@@ -417,7 +417,7 @@
         return p1y.at[n, both, both, zs_] if half == 0 else p1x.at[n, zs_]
 
     live[("nat", 1)].wait()
-    live[("dqk", 1)].wait()
+    finish("dqk", 2)
     for half in range(2):
         for l in range(2):
             at = half * 512 + l * 256
@@ -637,7 +637,7 @@
         mem((8, 2, *tile), F32), mem((7, 2, *tile), F32), mem((2, *tile), F32),
         mem((7, *tile), F32), mem(tile, F32), mem((3, *tile), F32), mem(tile, F32),
         mem((7, *tile), F32), mem(tile, F32), mem((7, *tile), F32),
-        dma((8,)), dma((31,)), dma((31,)), dma((1,)), dma((1,)), dma((1,)), dma((1,)),
+        dma((8,)), dma((32,)), dma((32,)), dma((1,)), dma((1,)), dma((1,)), dma((1,)),
         dma((59,)), dma((59,)), dma((28,)), dma((28,)),
     ]
     shapes = (

time: 85.1 us -> 88.3 us (1.038)
  Pallas kernels: 83.7 us -> 86.9 us
    pallas_call x1, Pallas kernels: 81.7 us -> 84.9 us  [per_device(): pl.pallas_call(kernel, out_shape=shapes, in_specs=[away, vmem, vmem, vmem...]
where the time goes in v5:
time: 88.3 us; the launch traced here: 88.2 us
  Pallas kernels  86.9 us (98%)
  between operations  1.29 us (1%)
    pallas_call x1, Pallas kernels, per_device(): pl.pallas_call(kernel, out_shape=shapes, in_specs=[away, vmem, vmem, vmem...  84.9 us
    pallas_call x1, Pallas kernels, per_device(): pl.pallas_call(hand_on, out_shape=shapes, in_specs=[vmem] * 4, out_specs=...  2 us

profile of v5, /device:TPU:1, one launch (start us, length us, event | category | flops | bytes accessed | tf_op | source)
XLA Modules:
  0.0 88.2 jit_solution(12073333479064153434)
XLA Ops:
  1.3 84.9 %shard_map.138 = (f32[4,64]{1,0:T(4,128)}, bf16[256,1024]{1,0:T(8,128)(2,1)}, f32[16,3072]{1,0:T(8,128)}, f32[16,1024]{1,0:T(8,128)}) custom-call(bf16[256,1024]{1,0:T(8,128)(2,1)} %bitcast.14, s32[1,1]{1,0:T(1,128)S(6)} %copy.15.done_v, s32[4,64]{1,0:T(4,128)} %bitcast.18, f32[4,64]{1,0:T(4,128)} %bitcast.19, f32[1,1024]{1,0:T(1,128)} %bitcast.15, ...), custom_call_target="tpu_custom_call" | custom-call | tf_op jit(solution)/shard_map/pallas_call | solution.py:649
  86.2 2.0 %shard_map.139 = (f32[4,64]{1,0:T(4,128)}, bf16[256,1024]{1,0:T(8,128)(2,1)}, f32[16,3072]{1,0:T(8,128)}, f32[16,1024]{1,0:T(8,128)}) custom-call(f32[4,64]{1,0:T(4,128)} %get-tuple-element.12.refs_0_, bf16[256,1024]{1,0:T(8,128)(2,1)} %get-tuple-element.13.refs_1_, f32[16,3072]{1,0:T(8,128)} %get-tuple-element.14.refs_2_, f32[16,1024]{1,0:T(8,128)} %get-tuple-element.15.refs_3_), custom_call_target="tpu_custom_call" | custom-call | tf_op jit(solution)/shard_map/pallas_call | solution.py:662

commit v6 on v5

--- a/solution.py
+++ b/solution.py
@@ -297,11 +297,10 @@
             recv_sem=sems[1].at[0], device_id=core_id, device_id_type=pl.DeviceIdType.MESH,
         ).wait()
 
+    z_1()
     g_3()
-    z_1()
     z_2()
     g_mid()
-    z_end()
     wait_all(a1, r1, (as1, ar1))
 
     unturn = block_to_agent(False)
@@ -321,8 +320,6 @@
     for j in range(4):
         nat[0, j * 256 : j * 256 + 256, :] = normed[:, j * 256 : j * 256 + 256].T.astype(BF16)
     begin("nat", 1, nat.at[0], nat.at[1], G, 29, core_id)
-    s_rows = nt(z128[0:32, :], na[...])
-    s_rows = s_rows[0:8] + s_rows[16:24]
     diag = ri == ci
     alive_f, target_f = alive_v[...].astype(F32), target_v[...]
 
@@ -346,6 +343,9 @@
     project(core)
     finish("gc", 8)
     project(1 - core)
+    z_end()
+    s_rows = nt(z128[0:32, :], na[...])
+    s_rows = s_rows[0:8] + s_rows[16:24]
     square = iota((128, 128), 0), iota((128, 128), 1)
     same_step = (square[0] // 64) == (square[1] // 64)
     sums = []

time: 88.3 us -> 85.4 us (0.967)
  Pallas kernels: 86.9 us -> 84 us
    pallas_call x1, Pallas kernels: 84.9 us -> 82 us  [per_device(): pl.pallas_call(kernel, out_shape=shapes, in_specs=[away, vmem, vmem, vmem...]
where the time goes in v6:
time: 85.4 us; the launch traced here: 85.3 us
  Pallas kernels  84 us (98%)
  between operations  1.29 us (2%)
    pallas_call x1, Pallas kernels, per_device(): pl.pallas_call(kernel, out_shape=shapes, in_specs=[away, vmem, vmem, vmem...  82 us
    pallas_call x1, Pallas kernels, per_device(): pl.pallas_call(hand_on, out_shape=shapes, in_specs=[vmem] * 4, out_specs=...  2 us

profile of v6, /device:TPU:1, one launch (start us, length us, event | category | flops | bytes accessed | tf_op | source)
XLA Modules:
  0.0 85.3 jit_solution(15342545735525803477)
XLA Ops:
  1.3 82.0 %shard_map.138 = (f32[4,64]{1,0:T(4,128)}, bf16[256,1024]{1,0:T(8,128)(2,1)}, f32[16,3072]{1,0:T(8,128)}, f32[16,1024]{1,0:T(8,128)}) custom-call(bf16[256,1024]{1,0:T(8,128)(2,1)} %bitcast.14, s32[1,1]{1,0:T(1,128)S(6)} %copy.15.done_v, s32[4,64]{1,0:T(4,128)} %bitcast.18, f32[4,64]{1,0:T(4,128)} %bitcast.19, f32[1,1024]{1,0:T(1,128)} %bitcast.15, ...), custom_call_target="tpu_custom_call" | custom-call | tf_op jit(solution)/shard_map/pallas_call | solution.py:649
  83.3 2.0 %shard_map.139 = (f32[4,64]{1,0:T(4,128)}, bf16[256,1024]{1,0:T(8,128)(2,1)}, f32[16,3072]{1,0:T(8,128)}, f32[16,1024]{1,0:T(8,128)}) custom-call(f32[4,64]{1,0:T(4,128)} %get-tuple-element.12.refs_0_, bf16[256,1024]{1,0:T(8,128)(2,1)} %get-tuple-element.13.refs_1_, f32[16,3072]{1,0:T(8,128)} %get-tuple-element.14.refs_2_, f32[16,1024]{1,0:T(8,128)} %get-tuple-element.15.refs_3_), custom_call_target="tpu_custom_call" | custom-call | tf_op jit(solution)/shard_map/pallas_call | solution.py:662

commit v7 on v6

--- a/solution.py
+++ b/solution.py
@@ -299,8 +299,8 @@
 
     z_1()
     g_3()
+    g_mid()
     z_2()
-    g_mid()
     wait_all(a1, r1, (as1, ar1))
 
     unturn = block_to_agent(False)

time: 85.4 us -> 85.3 us (level)
  no operation moved by 1% of the time
where the time goes in v7:
time: 85.3 us; the launch traced here: 85.2 us
  Pallas kernels  83.9 us (98%)
  between operations  1.29 us (2%)
    pallas_call x1, Pallas kernels, per_device(): pl.pallas_call(kernel, out_shape=shapes, in_specs=[away, vmem, vmem, vmem...  81.9 us
    pallas_call x1, Pallas kernels, per_device(): pl.pallas_call(hand_on, out_shape=shapes, in_specs=[vmem] * 4, out_specs=...  2 us

profile of v7, /device:TPU:1, one launch (start us, length us, event | category | flops | bytes accessed | tf_op | source)
XLA Modules:
  0.0 85.2 jit_solution(12981708051423746997)
XLA Ops:
  1.3 81.9 %shard_map.138 = (f32[4,64]{1,0:T(4,128)}, bf16[256,1024]{1,0:T(8,128)(2,1)}, f32[16,3072]{1,0:T(8,128)}, f32[16,1024]{1,0:T(8,128)}) custom-call(bf16[256,1024]{1,0:T(8,128)(2,1)} %bitcast.14, s32[1,1]{1,0:T(1,128)S(6)} %copy.15.done_v, s32[4,64]{1,0:T(4,128)} %bitcast.18, f32[4,64]{1,0:T(4,128)} %bitcast.19, f32[1,1024]{1,0:T(1,128)} %bitcast.15, ...), custom_call_target="tpu_custom_call" | custom-call | tf_op jit(solution)/shard_map/pallas_call | solution.py:649
  83.2 2.0 %shard_map.139 = (f32[4,64]{1,0:T(4,128)}, bf16[256,1024]{1,0:T(8,128)(2,1)}, f32[16,3072]{1,0:T(8,128)}, f32[16,1024]{1,0:T(8,128)}) custom-call(f32[4,64]{1,0:T(4,128)} %get-tuple-element.12.refs_0_, bf16[256,1024]{1,0:T(8,128)(2,1)} %get-tuple-element.13.refs_1_, f32[16,3072]{1,0:T(8,128)} %get-tuple-element.14.refs_2_, f32[16,1024]{1,0:T(8,128)} %get-tuple-element.15.refs_3_), custom_call_target="tpu_custom_call" | custom-call | tf_op jit(solution)/shard_map/pallas_call | solution.py:662
